TPU v7x, 32 devices: a whole 2x2x4 slice. The times are simulated.
32 devices in a mesh: gx: 4 (over z), gy: 8 (over y, x, core).
Axes of the slice: x: 2, y: 2, z: 4, core: 2. Of those that a mesh axis runs over, the one named last changes fastest.
Arguments:
- populations: float32 [27, 16, 128, 128], P(None, 'gx', 'gy'), may hold values from 0.01 to 0.07
- species: float32 [7, 20, 16, 128, 128], P(None, None, 'gx', 'gy'), may hold values from 0 to 0.4
- node_type: int32 [16, 128, 128], P('gx', 'gy'), may hold values from 0 to 3, as said below
- reactions: int32 [84, 3], replicated, may hold values from 0 to 19
- rate_const: float32 [84], replicated, may hold values from 0.005 to 0.05
- species_rate: float32 [20], replicated, may hold values from 0.7 to 1.8
- inlet_mix: float32 [2, 20], replicated, may hold values from 0 to 2
Outputs:
- new_populations: float32 [27, 16, 128, 128], P(None, 'gx', 'gy')
- new_species: float32 [7, 20, 16, 128, 128], P(None, None, 'gx', 'gy')
Inputs may be any that keep to these rules, and one draw needn't show every extreme that they name: `node_type`: rows y = 0 and y = 127 hold only walls and inlets: fuel inlets (2) in row 0 and oxidizer inlets (3) in row 127, for third coordinates from 32 to 95, walls elsewhere in these rows; other rows hold fluid (0) and scattered walls (1).
All inputs are finite; a program needn't handle non-finite values.
Results may differ from a plain program's by a relative error of at most 0.0001.
Values sent between devices are 32-bit elements; how exact they have to be, the bound alone decides.
No kernel may reach another device: no remote copies, remote signals or barrier semaphores. Data moves between devices by JAX's collectives and lax.ppermute only.
A program may use at most 128 MiB of HBM per device.

v0:
```python
import functools

import jax
import jax.numpy as jnp
from jax import lax
from jax.experimental import pallas as pl
from jax.experimental.pallas import tpu as pltpu
from jax.sharding import PartitionSpec as P


SUBSTEPS = 3
CONC = 10
OMEGA = 1.6
SPEED = 0.05
F32 = jnp.float32
BF16 = jnp.bfloat16
VEL = [(a, b, c) for a in (-1, 0, 1) for b in (-1, 0, 1) for c in (-1, 0, 1)]
WT = [(8.0 / 27, 2.0 / 27, 1.0 / 54, 1.0 / 216)[abs(a) + abs(b) + abs(c)] for a, b, c in VEL]
UPX = [q for q in range(27) if VEL[q][0] > 0]
DNX = [q for q in range(27) if VEL[q][0] < 0]
UPY = [q for q in range(27) if VEL[q][1] > 0]
DNY = [q for q in range(27) if VEL[q][1] < 0]
MIB = 1 << 20
VMEM = pltpu.VMEM
VM = pl.BlockSpec(memory_space=pltpu.VMEM)
SM = pl.BlockSpec(memory_space=pltpu.SMEM)
ANY = pl.BlockSpec(memory_space=pl.ANY)


def inv(x):
    return pltpu.with_memory_space_constraint(x, pltpu.VMEM)


def hbm(x):
    return pltpu.with_memory_space_constraint(x, pltpu.HBM)


def pairs(size, near):
    if near:
        return [(i, i ^ 1) for i in range(size)]
    return [(i, (i + 1 if i % 2 else i - 1) % size) for i in range(size)]


def is_even(axis):
    return lax.rem(lax.axis_index(axis), 2) == 0


def pick(even, one, other):
    return jnp.where(even, one, other)


class Halo:
    def __init__(self, near, far, axis):
        self.near, self.far, self.even = near, far, is_even(axis)

    def up(self, *at):
        return pick(self.even, self.far[at], self.near[at])

    def down(self, *at):
        return pick(self.even, self.near[at], self.far[at])


def call(body, ins, specs, outs, out_specs, scratch=(), alias=None, mib=12, cost=2_000_000):
    return pl.pallas_call(
        body,
        out_shape=outs,
        in_specs=specs,
        out_specs=out_specs,
        scratch_shapes=list(scratch),
        input_output_aliases=alias or {},
        compiler_params=pltpu.CompilerParams(vmem_limit_bytes=mib * MIB),
        cost_estimate=pl.CostEstimate(flops=cost, bytes_accessed=cost, transcendentals=0),
    )(*ins)


def react(rx, kc, c_ref, s_ref, w_ref, rt_ref, odd_ref=None, start=0, stop=None):
    species, rows, lanes = c_ref.shape
    part = slice(start, stop or rows)
    tiles = (part.stop - part.start) // 8
    half = w_ref.shape[1] // 2
    even = tiles - tiles % 2
    for i in range(half // 16):
        rates = []
        for n in range(2):
            j = 2 * i + n
            rates.append(c_ref[rx[0, j], part, :] * (c_ref[rx[1, j], part, :] * kc[j]))
        for t in range(tiles):
            both = jnp.concatenate([r[8 * t : 8 * t + 8] for r in rates], axis=0)
            high = both.astype(BF16)
            low = (both - high.astype(F32)).astype(BF16)
            if t < even:
                rt_ref[16 * i : 16 * i + 16, lanes * t : lanes * (t + 1)] = high
                rt_ref[half + 16 * i : half + 16 * i + 16, lanes * t : lanes * (t + 1)] = low
            else:
                odd_ref[16 * i : 16 * i + 16, :lanes] = high
                odd_ref[16 * i : 16 * i + 16, lanes:] = low
    if even < tiles:
        total = jnp.dot(w_ref[:, :half], odd_ref[...], preferred_element_type=F32)
        total = total[:, :lanes] + total[:, lanes:]
        s_ref[:, start + 8 * even : start + 8 * tiles, :] = total.reshape(species, 8, lanes)
    if even:
        total = jnp.dot(w_ref[...], rt_ref[:, : lanes * even], preferred_element_type=F32)
        for t in range(even):
            s_ref[:, start + 8 * t : start + 8 * t + 8, :] = total[
                :, lanes * t : lanes * (t + 1)
            ].reshape(species, 8, lanes)


def moments(f):
    rho = f[0]
    for q in range(1, 27):
        rho = rho + f[q]
    parts = []
    for axis in range(3):
        plus = None
        for q in range(27):
            if VEL[q][axis] > 0:
                diff = f[q] - f[26 - q]
                plus = diff if plus is None else plus + diff
        parts.append(plus)
    scale = 1.0 / rho
    return rho, [p * scale for p in parts]


def cross(g, rk, c, s, ux, sign):
    a = rk * c
    return (1.0 - rk) * g + (0.125 * (a + s) + (0.5 * sign) * (a * ux))


def bands(species):
    return [(k, min(8, species - k)) for k in range(0, species, 8)]


def stoichiometry(rv, w):
    rows, width = w.shape
    half = width // 2
    species, total = rows // 8, half // 8

    def iota(shape, axis):
        return lax.broadcasted_iota(jnp.int32, shape, axis)

    def hot(test):
        return jnp.where(test, 1.0, 0.0)

    label = iota((species, total), 0)
    net = hot(rv[2:3, :] == label) - hot(rv[0:1, :] == label) - hot(rv[1:2, :] == label)
    tall = hot((iota((rows, species), 0) >> 3) == iota((rows, species), 1)).astype(BF16)
    wide = hot((iota((total, half), 1) >> 3) == iota((total, half), 0)).astype(BF16)
    part = jnp.dot(tall, net.astype(BF16), preferred_element_type=F32)
    full = jnp.dot(part.astype(BF16), wide, preferred_element_type=F32)
    same = (iota((rows, half), 0) & 7) == (iota((rows, half), 1) & 7)
    full = jnp.where(same, full, 0.0).astype(BF16)
    w[:, :half] = full
    w[:, half:] = full


def first_body(pop, spec, react_in, kc_in, rk_in, mix_in, sv, w, ma, mb, ya, yb, c03, s03,
               fixed, u, post, rx, kc, rk, mix, rt, odd, keep, rv, psem, ssem, tsem, pv):
    planes, rows, lanes = pop.shape[1:]
    species = spec.shape[1]
    ends = (0, planes - 1)
    inner = range(1, planes - 1)
    small = [
        pltpu.make_async_copy(src, dst, tsem.at[n])
        for n, (src, dst) in enumerate(
            ((react_in, rv), (react_in, rx), (kc_in, kc), (rk_in, rk), (mix_in, mix))
        )
    ]
    kinds = [pltpu.make_async_copy(spec.at[:, :, x], sv.at[:, :, x], ssem.at[x])
             for x in range(planes)]
    flows = [pltpu.make_async_copy(pop.at[:, x], pv.at[:, x], psem.at[x]) for x in range(planes)]
    for copy in small + [kinds[x] for x in ends] + flows + [kinds[x] for x in inner]:
        copy.start()
    for k in range(species):
        c03[k, 2 * rows :, :] = jnp.zeros((c03.shape[1] - 2 * rows, lanes), F32)
    for copy in small:
        copy.wait()
    stoichiometry(rv, w)
    for k in range(species):
        for n, value in enumerate((rk[k], mix[0, k], mix[1, k])):
            fixed[n, k : k + 1, :] = jnp.full((1, lanes), value, F32)
    for side in range(2):
        for n, i in enumerate((0, 1, 3, 4)):
            fixed[3 + 4 * side + n] = inlet_weight(i, side) * fixed[1 + side]
    for n, x in enumerate(ends):
        kinds[x].wait()

        def conc(k, carry, n=n, x=x):
            total = sv[0, k, x]
            for i in range(1, 7):
                total = total + sv[i, k, x]
            c03[k, n * rows : (n + 1) * rows, :] = total
            return carry

        lax.fori_loop(0, species, conc, 0, unroll=5)
    react(rx, kc, c03, s03, w, rt, start=0, stop=2 * rows)
    for copy in flows:
        copy.wait()
    collide_flow(pv, u, post)
    for x in inner:
        kinds[x].wait()
    flat = sv.reshape(7 * species * planes * rows, lanes)
    height = c03.shape[1]
    cflat = c03.reshape(species * height, lanes)
    for x in inner:
        for side, row in ((0, 0), (1, rows - 1)):
            for k, size in bands(species):
                values = [
                    flat[pl.ds(((i * species + k) * planes + x) * rows + row, size, planes * rows), :]
                    for i in range(7)
                ]
                total = values[0]
                for i in range(1, 7):
                    total = total + values[i]
                spot = 2 * rows + 2 * (x - 1) + side
                cflat[pl.ds(k * height + spot, size, height), :] = total
                keep[side, x * species + k : x * species + k + size, :] = values[3 if side else 4]
    react(rx, kc, c03, s03, w, rt, odd, start=2 * rows)
    send_faces(sv, rk, c03, s03, [u[0, x] for x in ends], ma, mb)
    send_rows(sv, keep, c03, s03, fixed, u, ya, yb)
    first, last, even = edge_flags()
    for n in range(9):
        for x in range(planes):
            at = slice((species + n) * planes + x, (species + n) * planes + x + 1)
            top = jnp.where(last, 0.0, post[UPY[n], x, rows - 1 : rows, :])
            bottom = jnp.where(first, 0.0, post[DNY[n], x, 0:1, :])
            ya[at, :] = pick(even, top, bottom)
            yb[at, :] = pick(even, bottom, top)


def edge_flags():
    rank, size = lax.axis_index("gy"), lax.axis_size("gy")
    return rank == 0, rank == size - 1, is_even("gy")


def send_rows(state, keep, c03, s03, fixed, u, ya, yb):
    species, planes, rows, lanes = state.shape[1:]
    height = c03.shape[1]
    fresh = state.reshape(7 * species * planes * rows, lanes)
    cflat = c03.reshape(species * height, lanes)
    sflat = s03.reshape(species * height, lanes)
    first, last, even = edge_flags()
    for x in range(planes):
        for k, size in bands(species):
            halo = slice(x * species + k, x * species + k + size)
            sent = []
            for side, row, off in ((0, 0, first), (1, rows - 1, last)):
                i, sign = (3, 1.0) if side else (4, -1.0)
                if x in (0, planes - 1):
                    spot = (x > 0) * rows + row
                    at = ((i * species + k) * planes + x) * rows + row
                    value = fresh[pl.ds(at, size, planes * rows), :]
                else:
                    spot = 2 * rows + 2 * (x - 1) + side
                    value = keep[side, halo, :]
                c = cflat[pl.ds(k * height + spot, size, height), :]
                s = sflat[pl.ds(k * height + spot, size, height), :]
                uy = u[1, x, row : row + 1, :]
                value = cross(value, fixed[0, k : k + size, :], c, s, uy, sign)
                sent.append(jnp.where(off, 0.0, value))
            ya[halo, :] = pick(even, sent[1], sent[0])
            yb[halo, :] = pick(even, sent[0], sent[1])


def send_faces(state, rk, c03, s03, speeds, ma, mb):
    species, planes, rows = state.shape[1:4]
    even = is_even("gx")

    def send(k, carry):
        low = cross(state[2, k, 0], rk[k], c03[k, :rows, :], s03[k, :rows, :], speeds[0], -1.0)
        part = slice(rows, 2 * rows)
        high = cross(
            state[1, k, planes - 1], rk[k], c03[k, part, :], s03[k, part, :], speeds[1], 1.0
        )
        ma[k] = pick(even, high, low)
        mb[k] = pick(even, low, high)
        return carry

    lax.fori_loop(0, species, send, 0, unroll=5)


def relaxed(rho, v, q):
    still = 1.0 - 1.5 * (v[0] * v[0] + v[1] * v[1] + v[2] * v[2])
    along = None
    for axis in range(3):
        if VEL[q][axis]:
            term = v[axis] if VEL[q][axis] > 0 else -v[axis]
            along = term if along is None else along + term
    return still, OMEGA * rho, (still + 4.5 * along * along, 3.0 * along)


def collide_flow(pv, u, post):
    for x in range(pv.shape[1]):
        f = [pv[q, x] for q in range(27)]
        rho, v = moments(f)
        for axis in range(3):
            u[axis, x] = v[axis]
        for q in range(14, 27):
            still, scaled, (even, odd) = relaxed(rho, v, q)
            ws = WT[q] * scaled
            for p, value in ((q, even + odd), (26 - q, even - odd)):
                post[p, x] = (1.0 - OMEGA) * f[p] + ws * value
        post[13, x] = (1.0 - OMEGA) * f[13] + WT[13] * scaled * still


def row_index(rows, lanes):
    return lax.broadcasted_iota(jnp.int32, (rows, lanes), 0)


def gather(k, x, g, hx, hy, pairs):
    species, planes, rows, lanes = g.shape[1:]
    out = {}
    if 0 in pairs:
        out[0] = g[0, k, x]
    if 1 in pairs:
        out[1] = g[1, k, x - 1] if x > 0 else hx.up(k)
        out[2] = g[2, k, x + 1] if x < planes - 1 else hx.down(k)
    if 3 in pairs:
        flat = g.reshape(7 * species * planes * rows, lanes)
        at = row_index(8, lanes)
        spot = pl.ds(x * species + k, 1)
        for i, step, halo in ((3, -1, hy.up), (4, 1, hy.down)):
            base = ((i * species + k) * planes + x) * rows + step
            parts = [flat[pl.ds(base + t, 8), :] for t in range(0, rows, 8)]
            edge, row = (0, 0) if step < 0 else (-1, 7)
            parts[edge] = jnp.where(at == row, halo(spot, slice(None)), parts[edge])
            out[i] = jnp.concatenate(parts, axis=0)
    if 5 in pairs:
        out[5] = pltpu.roll(g[5, k, x], 1, 1)
        out[6] = pltpu.roll(g[6, k, x], lanes - 1, 1)
    return out


def masks(nt, x):
    rows = nt.shape[1]
    return nt[x] == 1, nt[x, :8, :] == 2, nt[x, rows - 8 :, :] == 3


def settle(value, kind, k, fixed, base):
    _, low, high = kind
    spot = pl.ds(k, 1)
    first = jnp.where(low, fixed[base[0], spot, :], value[:8])
    if value.shape[0] == 8:
        return jnp.where(high, fixed[base[1], spot, :], first)
    last = jnp.where(high, fixed[base[1], spot, :], value[-8:])
    return jnp.concatenate([first, value[8:-8], last] if value.shape[0] > 16 else [first, last], 0)


def walled(moved, kind, k, fixed):
    swap = (0, 2, 1, 4, 3, 6, 5)
    out = {}
    for i, m in moved.items():
        n = {0: 0, 3: 2, 4: 3}.get(i, 1)
        value = m if i == 0 else jnp.where(kind[0], moved[swap[i]], m)
        out[i] = settle(value, kind, k, fixed, (3 + n, 7 + n))
    return out


def inlet_weight(i, side):
    tilt = 4.0 * SPEED * (1.0 if side == 0 else -1.0)
    return {0: 0.25, 3: 0.125 * (1.0 + tilt), 4: 0.125 * (1.0 - tilt)}.get(i, 0.125)


def edge_body(g, hxa, hxb, hya, hyb, nt, u, rx, kc, rk, w, fixed, new, ma, mb, ya, yb, c03, s03,
              rt, odd, keep):
    hx, hy = Halo(hxa, hxb, "gx"), Halo(hya, hyb, "gy")
    species, planes, rows, lanes = g.shape[1:]
    height = c03.shape[1]
    ends = (0, planes - 1)
    flat = g.reshape(7 * species * planes * rows, lanes)
    cflat = c03.reshape(species * height, lanes)
    jump = planes * rows
    zeros = height - 2 * rows
    for k in range(species):
        c03[k, 2 * rows :, :] = jnp.zeros((zeros, lanes), F32)
    for x in range(1, planes - 1):
        for side, row in ((0, 0), (1, rows - 1)):
            kind = nt[x, row : row + 1, :]
            for k, size in bands(species):

                def load(i, plane, r, k=k, size=size):
                    return flat[pl.ds(((i * species + k) * planes + plane) * rows + r, size, jump), :]

                halo = slice(x * species + k, x * species + k + size)
                moved = {
                    0: load(0, x, row),
                    1: load(1, x - 1, row),
                    2: load(2, x + 1, row),
                    3: hy.up(halo, slice(None)) if side == 0 else load(3, x, row - 1),
                    4: hy.down(halo, slice(None)) if side == 1 else load(4, x, row + 1),
                    5: pltpu.roll(load(5, x, row), 1, 1),
                    6: pltpu.roll(load(6, x, row), lanes - 1, 1),
                }
                wide = jnp.broadcast_to(kind, (size, lanes))
                inlet = wide == 2 + side
                value = fixed[1 + side, k : k + size, :]
                total = moved[0]
                for i in range(1, 7):
                    total = total + moved[i]
                total = jnp.where(inlet, value, total)
                i = 3 if side else 4
                kept = jnp.where(wide == 1, moved[7 - i], moved[i])
                kept = jnp.where(inlet, inlet_weight(i, side) * value, kept)
                spot = 2 * rows + 2 * (x - 1) + side
                cflat[pl.ds(k * height + spot, size, height), :] = total
                keep[side, halo, :] = kept
    for n, x in enumerate(ends):
        kind = masks(nt, x)

        def step(k, carry, n=n, x=x, kind=kind):
            moved = gather(k, x, g, hx, hy, (0, 1, 3, 5))
            values = walled(moved, kind, k, fixed)
            total = moved[0]
            for i in range(1, 7):
                total = total + moved[i]
            for i in range(7):
                new[i, k, x] = values[i]
            c03[k, n * rows : (n + 1) * rows, :] = settle(total, kind, k, fixed, (1, 2))
            return carry

        lax.fori_loop(0, species, step, 0, unroll=CONC)
    react(rx, kc, c03, s03, w, rt, odd)
    send_faces(new, rk, c03, s03, [u[0, x] for x in ends], ma, mb)
    send_rows(new, keep, c03, s03, fixed, u, ya, yb)


def rest_body(moving, *refs):
    refs = list(refs)
    g = refs.pop(0) if moving else None
    start, c03, s03, u, rx, kc, rk, w = [refs.pop(0) for _ in range(8)]
    if moving:
        hya, hyb, nt, fixed = [refs.pop(0) for _ in range(4)]
        hy = Halo(hya, hyb, "gy")
    new, c12, s12, rt = refs
    species, planes, rows, _ = new.shape[1:]
    for x in range(1, planes - 1):
        kind = masks(nt, x) if moving else None

        def step(k, carry, x=x, kind=kind):
            if moving:
                moved = gather(k, x, g, None, hy, (0, 1, 3, 5))
                values = walled(moved, kind, k, fixed)
            else:
                moved = {i: start[i, k, x] for i in range(7)}
            total = moved[0]
            for i in range(1, 7):
                total = total + moved[i]
            if moving:
                for i in range(7):
                    new[i, k, x] = values[i]
                total = settle(total, kind, k, fixed, (1, 2))
            c12[k, (x - 1) * rows : x * rows, :] = total
            return carry

        lax.fori_loop(0, species, step, 0, unroll=CONC)
    react(rx, kc, c12, s12, w, rt)
    for x in range(planes):
        ux, uy, uz = 0.5 * u[0, x], 0.5 * u[1, x], 0.5 * u[2, x]
        if x in (0, planes - 1):
            cr, sr, half = c03, s03, slice((x > 0) * rows, (x > 0) * rows + rows)
        else:
            cr, sr, half = c12, s12, slice((x - 1) * rows, x * rows)

        def collide(k, carry, x=x, cr=cr, sr=sr, half=half, ux=ux, uy=uy, uz=uz):
            r = rk[k]
            keep = 1.0 - r
            a = r * cr[k, half, :]
            base1 = 0.125 * (a + sr[k, half, :])
            new[0, k, x] = keep * new[0, k, x] + (base1 + base1)
            for i, v in ((1, ux), (3, uy), (5, uz)):
                d = a * v
                up = keep * new[i, k, x] + (base1 + d)
                down = keep * new[i + 1, k, x] + (base1 - d)
                new[i, k, x] = up
                new[i + 1, k, x] = down
            return carry

        lax.fori_loop(0, species, collide, 0, unroll=5)


def faces_body(species, post, hya, hyb, fa, fb):
    planes = post.shape[1]
    hy = Halo(hya, hyb, "gy")
    even = is_even("gx")
    for n in range(9):
        high = flow_moved(UPX[n], planes - 1, post, hy, species * planes)
        low = flow_moved(DNX[n], 0, post, hy, species * planes)
        fa[n] = pick(even, high, low)
        fb[n] = pick(even, low, high)


def flow_moved(q, src, post, hy, base):
    planes, rows, lanes = post.shape[1:]
    at = row_index(rows, lanes)
    step = VEL[q][1]
    value = post[q, src]
    if step:
        row, queue, halo = (0, UPY, hy.up) if step > 0 else (rows - 1, DNY, hy.down)
        spot = base + queue.index(q) * planes + src
        shifted = pltpu.roll(value, step % rows, 0)
        value = jnp.where(at == row, halo(slice(spot, spot + 1), slice(None)), shifted)
    return value


def flow_end_body(species, post, fxa, fxb, hya, hyb, nt, result, out, sem):
    planes, _, lanes = post.shape[1:]
    base = species * planes
    hx, hy = Halo(fxa, fxb, "gx"), Halo(hya, hyb, "gy")
    copies = []
    for x in list(range(1, planes - 1)) + [0, planes - 1]:
        kind = nt[x]
        wall = kind == 1
        inlet = kind >= 2
        fuel = kind == 2
        for q in range(13, 27):
            moved = {}
            for p in {q, 26 - q}:
                a, _, c = VEL[p]
                src = x - a
                if src < 0:
                    value = hx.up(UPX.index(p))
                elif src >= planes:
                    value = hx.down(DNX.index(p))
                else:
                    value = flow_moved(p, src, post, hy, base)
                if c:
                    value = pltpu.roll(value, 1 if c > 0 else lanes - 1, 1)
                moved[p] = value
            for p in moved:
                cu = VEL[p][1] * SPEED
                fixed = [
                    WT[p] * (1.0 + 3.0 * s * cu + 4.5 * cu * cu - 1.5 * SPEED * SPEED)
                    for s in (1.0, -1.0)
                ]
                value = moved[p] if p == 13 else jnp.where(wall, moved[26 - p], moved[p])
                out[p, x] = jnp.where(inlet, jnp.where(fuel, fixed[0], fixed[1]), value)
        copies.append(pltpu.make_async_copy(out.at[:, x], result.at[:, x], sem.at[x]))
        copies[-1].start()
    for copy in copies:
        copy.wait()


def end_body(mode, *refs):
    refs = list(refs)
    g = refs.pop(0)
    hx = Halo(refs.pop(0), refs.pop(0), "gx") if mode == 1 else None
    hy = Halo(refs.pop(0), refs.pop(0), "gy") if mode == 3 else None
    nt, fixed = [refs.pop(0) for _ in range(2)]
    if mode:
        refs.pop(0)
    out, buf, sem = refs
    species, planes = g.shape[1:3]
    inner = range(1, planes - 1)
    cover = {
        0: {0: range(planes), 5: range(planes), 1: inner},
        3: {3: range(planes)},
        1: {1: (0, planes - 1)},
    }[mode]
    chunk = 5 if species % 5 == 0 else 1
    copies = []
    for start in range(0, species, chunk):
        for x in range(planes):
            pairs = [p for p, xs in cover.items() if x in xs]
            if not pairs:
                continue
            kind = masks(nt, x)

            def step(k, carry, x=x, pairs=pairs, kind=kind):
                values = walled(gather(k, x, g, hx, hy, pairs), kind, k, fixed)
                for i, value in values.items():
                    buf[i - mode, k, x] = value
                return carry

            lax.fori_loop(start, start + chunk, step, 0, unroll=True)
        part = slice(start, start + chunk)
        for pair in cover:
            for i in (0,) if pair == 0 else (pair, pair + 1):
                if pair != 1:
                    spans = [slice(0, planes)]
                elif mode == 0:
                    spans = [slice(1, planes - 1)]
                else:
                    spans = [slice(0, 1), slice(planes - 1, planes)]
                for span in spans:
                    copies.append(
                        pltpu.make_async_copy(
                            buf.at[i - mode, part, span], out.at[i, part, span], sem.at[len(copies)]
                        )
                    )
                    copies[-1].start()
    for copy in copies:
        copy.wait()


def per_device(populations, species, node_type, reactions, rate_const, species_rate, inlet_mix):
    planes, rows, lanes = node_type.shape
    count = species.shape[1]
    total = reactions.shape[0]
    pad = total % 2
    if pad:
        reactions = jnp.pad(reactions, ((0, pad), (0, 0)))
        rate_const = jnp.pad(rate_const, (0, pad))
        total += pad
    nt = inv(node_type)
    smem = [SM] * 3

    def arr(*shape):
        return VMEM(shape, F32)

    state = arr(7, count, planes, rows, lanes)
    inner = planes - 2
    edges = -(-2 * inner // 8) * 8
    wide = (2 * rows + edges) // 8
    react_out = arr(count, 2 * rows + edges, lanes)
    rates = VMEM((2 * total * 8, wide // 2 * 2 * lanes), BF16)
    odd = VMEM((total * 8, 2 * lanes), BF16)
    rates_in = VMEM((2 * total * 8, inner * rows // 8 * lanes), BF16)
    inside = VMEM((count, inner * rows, lanes), F32)

    def swap(near, far, axis):
        size = lax.axis_size(axis)
        far = lax.ppermute(far, axis, pairs(size, False))
        near = lax.ppermute(near, axis, pairs(size, True))
        return near, far

    xmsg = arr(count, rows, lanes)
    sems = [pltpu.SemaphoreType.DMA((planes,)), pltpu.SemaphoreType.DMA((planes,))]
    ints = pltpu.SMEM((3, total), jnp.int32)
    flows = arr(27, planes, rows, lanes)
    ymsg = arr((count + 9) * planes, lanes)
    keep = VMEM((2, count * planes, lanes), F32)
    sv, w, ma, mb, ya, yb, c03, s03, fixed, u, post, *tables = call(
        first_body,
        [hbm(v) for v in (populations, species, reactions.T, rate_const, species_rate, inlet_mix)],
        [ANY] * 6,
        (flows, state, VMEM((count * 8, 2 * total * 8), BF16), xmsg, xmsg, ymsg, ymsg, react_out,
         react_out, arr(11, count, lanes), arr(3, planes, rows, lanes), flows, ints,
         pltpu.SMEM((total,), F32), pltpu.SMEM((count,), F32))[1:],
        [VM] * 11 + [SM] * 3,
        [pltpu.SMEM((2, count), F32), rates, odd, keep, VMEM((3, total), jnp.int32)] + sems
        + [pltpu.SemaphoreType.DMA((5,)), flows],
    )
    tables = [pltpu.with_memory_space_constraint(v, pltpu.SMEM) for v in tables]
    hx = swap(ma, mb, "gx")
    hy = swap(ya, yb, "gy")
    ymsg = arr(count * planes, lanes)
    flow_hy = hy
    g = None
    new = sv
    for s in range(SUBSTEPS):
        moving = s > 0
        if moving:
            halo = hy
            new, ma, mb, ya, yb, c03, s03 = call(
                edge_body,
                [inv(v) for v in (g, *hx, *hy, node_type, u)] + tables + [inv(w), inv(fixed)],
                [VM] * 7 + smem + [VM] * 2,
                (state, xmsg, xmsg, ymsg, ymsg, react_out, react_out),
                [VM] * 7,
                [rates, odd, keep],
            )
            hx = swap(ma, mb, "gx")
            hy = swap(ya, yb, "gy")
        ins = ([inv(g)] if moving else []) + [inv(v) for v in (new, c03, s03, u)]
        ins += tables + [inv(w)]
        specs = [VM] * (5 if moving else 4) + smem + [VM]
        if moving:
            ins += [inv(v) for v in (*halo, node_type, fixed)]
        specs += [VM] * (len(ins) - len(specs))
        (g,) = call(
            functools.partial(rest_body, moving),
            ins,
            specs,
            (state,),
            [VM],
            [inside, inside, rates_in],
            alias={1 if moving else 0: 0},
        )
        if not moving:
            face = arr(9, rows, lanes)
            sent = call(
                functools.partial(faces_body, count),
                [inv(v) for v in (post, *hy)],
                [VM] * 3,
                (face, face),
                [VM] * 2,
            )
            flow_hx = swap(*sent, "gx")
    new_populations = call(
        functools.partial(flow_end_body, count),
        [inv(v) for v in (post, *flow_hx, *flow_hy, node_type)],
        [VM] * 6,
        pltpu.HBM((27, planes, rows, lanes), F32),
        ANY,
        [flows, sems[0]],
    )
    result = None
    for mode, extra in ((0, ()), (3, hy), (1, hx)):
        ins = [inv(v) for v in (g,) + extra] + [nt, inv(fixed)] + ([hbm(result)] if mode else [])
        result = call(
            functools.partial(end_body, mode),
            ins,
            [VM] * (3 + len(extra)) + ([ANY] if mode else []),
            pltpu.HBM((7, count, planes, rows, lanes), F32),
            ANY,
            [VMEM((7 if mode == 0 else 2, count, planes, rows, lanes), F32),
             pltpu.SemaphoreType.DMA((32,))],
            alias={len(ins) - 1: 0} if mode else None,
        )
    return new_populations, result


def solution(mesh):
    flow = P(None, "gx", "gy", None)
    kinds = P(None, None, "gx", "gy", None)
    return jax.shard_map(
        per_device,
        mesh=mesh,
        in_specs=(flow, kinds, P("gx", "gy", None), P(), P(), P(), P()),
        out_specs=(flow, kinds),
        check_vma=False,
    )
```

profile of v0, /device:TPU:1, one launch (start us, length us, event | category | flops | bytes accessed | tf_op | source)
XLA Modules:
  0.0 50.2 jit_solution(8067512024561628724)
XLA Ops:
  0.6 3.9 %shard_map.86 = (f32[7,20,4,16,128]{4,3,2,1,0:T(8,128)S(1)}, bf16[160,1344]{1,0:T(8,128)(2,1)S(1)}, f32[20,16,128]{2,1,0:T(8,128)S(1)}, f32[20,16,128]{2,1,0:T(8...) custom-call(f32[27,4,16,128]{3,2,1,0:T(8,128)} %pop.1, ...), custom_call_target="tpu_custom_call" | custom-call | flops 2000000 | bytes 2000000 | tf_op jit(solution)/shard_map/pallas_call | solution.py:64
  4.5 2.2 %collective-permute-start.4 = (f32[20,16,128]{2,1,0:T(8,128)S(1)}, f32[20,16,128]{2,1,0:T(8,128)S(1)}, u32[]{:S(2)}, u32[]{:S(2)}) collective-permute-start(f32[20,16,128]{2,1,0:T(8,128)S(1)} %get-tuple-element.45), channel_id=1, source_target_pairs={{0,8},{8,0},{16,24},{24,16},{1,9},{9,1},{17,25},{25,17},{2,10},{10... | collective-permute-start | bytes 491528 | tf_op jit(solution)/shard_map/ppermute | solution.py:623
  6.7 2.2 %collective-permute-start.5 = (f32[20,16,128]{2,1,0:T(8,128)S(1)}, f32[20,16,128]{2,1,0:T(8,128)S(1)}, u32[]{:S(2)}, u32[]{:S(2)}) collective-permute-start(f32[20,16,128]{2,1,0:T(8,128)S(1)} %get-tuple-element.46), channel_id=1, source_target_pairs={{0,24},{8,16},{16,8},{24,0},{1,25},{9,17},{17,9},{25,1},{2,26},{10... | collective-permute-start | bytes 491528 | tf_op jit(solution)/shard_map/ppermute | solution.py:622
  8.9 1.2 %collective-permute-start = (f32[116,128]{1,0:T(8,128)S(1)}, f32[116,128]{1,0:T(8,128)S(1)}, u32[]{:S(2)}, u32[]{:S(2)}) collective-permute-start(f32[116,128]{1,0:T(8,128)S(1)} %get-tuple-element.33), channel_id=1, source_target_pairs={{0,1},{1,0},{2,3},{3,2},{4,5},{5,4},{6,7},{7,6},{8,9},{9,8},{10,11... | collective-permute-start | bytes 178184 | tf_op jit(solution)/shard_map/ppermute | solution.py:623
  10.1 1.1 %collective-permute-start.1 = (f32[116,128]{1,0:T(8,128)S(1)}, f32[116,128]{1,0:T(8,128)S(1)}, u32[]{:S(2)}, u32[]{:S(2)}) collective-permute-start(f32[116,128]{1,0:T(8,128)S(1)} %get-tuple-element.34), channel_id=1, source_target_pairs={{0,7},{1,2},{2,1},{3,4},{4,3},{5,6},{6,5},{7,0},{8,15},{9,10},{10,... | collective-permute-start | bytes 178184 | tf_op jit(solution)/shard_map/ppermute | solution.py:622
  11.2 1.6 %shard_map.89.g.refs_0_ = f32[7,20,4,16,128]{4,3,2,1,0:T(8,128)S(1)} custom-call(f32[7,20,4,16,128]{4,3,2,1,0:T(8,128)S(1)} %get-tuple-element.37.refs_0_, f32[20,40,128]{2,1,0:T(8,128)S(1)} %get-tuple-element.38.refs_1_, f32[20,40,128]{2,1,0:T(8,128)S(1)} %get-tuple-element.39.refs_2_, ...), custom_call_target="tpu_custom_call", output_to_operand_aliasing={{}: (0, {})} | custom-call | flops 2000000 | bytes 2000000 | tf_op jit(solution)/shard_map/pallas_call | solution.py:64
  12.9 0.0 collective-permute-done.hya.refs_9_
  12.9 1.4 %collective-permute-done.1.hyb.refs_10_ = f32[116,128]{1,0:T(8,128)S(1)} collective-permute-done((f32[116,128]{1,0:T(8,128)S(1)}, f32[116,128]{1,0:T(8,128)S(1)}, u32[]{:S(2)}, u32[]{:S(2)}) %collective-permute-start.1) | collective-permute-done | bytes 59424 | tf_op jit(solution)/shard_map/ppermute | solution.py:622
  14.3 0.0 collective-permute-done.4.hxa
  14.3 1.8 %collective-permute-done.5.hxb = f32[20,16,128]{2,1,0:T(8,128)S(1)} collective-permute-done((f32[20,16,128]{2,1,0:T(8,128)S(1)}, f32[20,16,128]{2,1,0:T(8,128)S(1)}, u32[]{:S(2)}, u32[]{:S(2)}) %collective-permute-start.5) | collective-permute-done | bytes 163872 | tf_op jit(solution)/shard_map/ppermute | solution.py:622
  16.1 1.7 %shard_map.90 = (f32[7,20,4,16,128]{4,3,2,1,0:T(8,128)S(1)}, f32[20,16,128]{2,1,0:T(8,128)S(1)}, f32[20,16,128]{2,1,0:T(8,128)S(1)}, f32[80,128]{1,0:T(8,128)S(1...) custom-call(f32[7,20,4,16,128]{4,3,2,1,0:T(8,128)S(1)} %shard_map.89.g.refs_0_, ...), custom_call_target="tpu_custom_call" | custom-call | flops 2000000 | bytes 2000000 | tf_op jit(solution)/shard_map/pallas_call | solution.py:64
  17.8 0.1 collective-permute-start.6
  17.9 2.6 %collective-permute-start.7 = (f32[20,16,128]{2,1,0:T(8,128)S(1)}, f32[20,16,128]{2,1,0:T(8,128)S(1)}, u32[]{:S(2)}, u32[]{:S(2)}) collective-permute-start(f32[20,16,128]{2,1,0:T(8,128)S(1)} %get-tuple-element.52), channel_id=1, source_target_pairs={{0,24},{8,16},{16,8},{24,0},{1,25},{9,17},{17,9},{25,1},{2,26},{10... | collective-permute-start | bytes 491528 | tf_op jit(solution)/shard_map/ppermute | solution.py:622
  20.5 2.2 %collective-permute-start.8 = (f32[80,128]{1,0:T(8,128)S(1)}, f32[80,128]{1,0:T(8,128)S(1)}, u32[]{:S(2)}, u32[]{:S(2)}) collective-permute-start(f32[80,128]{1,0:T(8,128)S(1)} %get-tuple-element.53), channel_id=1, source_target_pairs={{0,1},{1,0},{2,3},{3,2},{4,5},{5,4},{6,7},{7,6},{8,9},{9,8},{10,11... | collective-permute-start | bytes 122888 | tf_op jit(solution)/shard_map/ppermute | solution.py:623
  22.6 1.1 %collective-permute-start.9 = (f32[80,128]{1,0:T(8,128)S(1)}, f32[80,128]{1,0:T(8,128)S(1)}, u32[]{:S(2)}, u32[]{:S(2)}) collective-permute-start(f32[80,128]{1,0:T(8,128)S(1)} %get-tuple-element.54), channel_id=1, source_target_pairs={{0,7},{1,2},{2,1},{3,4},{4,3},{5,6},{6,5},{7,0},{8,15},{9,10},{10,... | collective-permute-start | bytes 122888 | tf_op jit(solution)/shard_map/ppermute | solution.py:622
  23.7 2.0 %shard_map.91.g.refs_0_ = f32[7,20,4,16,128]{4,3,2,1,0:T(8,128)S(1)} custom-call(f32[7,20,4,16,128]{4,3,2,1,0:T(8,128)S(1)} %shard_map.89.g.refs_0_, f32[7,20,4,16,128]{4,3,2,1,0:T(8,128)S(1)} %get-tuple-element.48.refs_1_, f32[20,40,128]{2,1,0:T(8,128)S(1)} %get-tuple-element.49.refs_2_, ...), custom_call_target="tpu_custom_call", output_to_operand_aliasing={{}: (1, {})} | custom-call | flops 2000000 | bytes 2000000 | tf_op jit(solution)/shard_map/pallas_call | solution.py:64
  25.7 0.8 %collective-permute-done.9.hyb.refs_10_ = f32[80,128]{1,0:T(8,128)S(1)} collective-permute-done((f32[80,128]{1,0:T(8,128)S(1)}, f32[80,128]{1,0:T(8,128)S(1)}, u32[]{:S(2)}, u32[]{:S(2)}) %collective-permute-start.9) | collective-permute-done | bytes 40992 | tf_op jit(solution)/shard_map/ppermute | solution.py:622
  26.5 1.7 %shard_map.92 = (f32[7,20,4,16,128]{4,3,2,1,0:T(8,128)S(1)}, f32[20,16,128]{2,1,0:T(8,128)S(1)}, f32[20,16,128]{2,1,0:T(8,128)S(1)}, f32[80,128]{1,0:T(8,128)S(1...) custom-call(f32[7,20,4,16,128]{4,3,2,1,0:T(8,128)S(1)} %shard_map.91.g.refs_0_, ...), custom_call_target="tpu_custom_call" | custom-call | flops 2000000 | bytes 2000000 | tf_op jit(solution)/shard_map/pallas_call | solution.py:64
  28.2 0.1 collective-permute-start.10
  28.3 2.0 %collective-permute-start.11 = (f32[20,16,128]{2,1,0:T(8,128)S(1)}, f32[20,16,128]{2,1,0:T(8,128)S(1)}, u32[]{:S(2)}, u32[]{:S(2)}) collective-permute-start(f32[20,16,128]{2,1,0:T(8,128)S(1)} %get-tuple-element.59), channel_id=1, source_target_pairs={{0,24},{8,16},{16,8},{24,0},{1,25},{9,17},{17,9},{25,1},{2,26},{10... | collective-permute-start | bytes 491528 | tf_op jit(solution)/shard_map/ppermute | solution.py:622
  30.4 0.6 %collective-permute-start.2 = (f32[9,16,128]{2,1,0:T(8,128)S(1)}, f32[9,16,128]{2,1,0:T(8,128)S(1)}, u32[]{:S(2)}, u32[]{:S(2)}) collective-permute-start(f32[9,16,128]{2,1,0:T(8,128)S(1)} %get-tuple-element.35), channel_id=1, source_target_pairs={{0,8},{8,0},{16,24},{24,16},{1,9},{9,1},{17,25},{25,17},{2,10},{10... | collective-permute-start | bytes 221192 | tf_op jit(solution)/shard_map/ppermute | solution.py:623
  30.9 1.3 %collective-permute-start.3 = (f32[9,16,128]{2,1,0:T(8,128)S(1)}, f32[9,16,128]{2,1,0:T(8,128)S(1)}, u32[]{:S(2)}, u32[]{:S(2)}) collective-permute-start(f32[9,16,128]{2,1,0:T(8,128)S(1)} %get-tuple-element.36), channel_id=1, source_target_pairs={{0,24},{8,16},{16,8},{24,0},{1,25},{9,17},{17,9},{25,1},{2,26},{10... | collective-permute-start | bytes 221192 | tf_op jit(solution)/shard_map/ppermute | solution.py:622
  32.2 3.8 %collective-permute-start.12 = (f32[80,128]{1,0:T(8,128)S(1)}, f32[80,128]{1,0:T(8,128)S(1)}, u32[]{:S(2)}, u32[]{:S(2)}) collective-permute-start(f32[80,128]{1,0:T(8,128)S(1)} %get-tuple-element.60), channel_id=1, source_target_pairs={{0,1},{1,0},{2,3},{3,2},{4,5},{5,4},{6,7},{7,6},{8,9},{9,8},{10,11... | collective-permute-start | bytes 122888 | tf_op jit(solution)/shard_map/ppermute | solution.py:623
  36.1 0.2 collective-permute-done.2.fxa
  36.3 6.4 %collective-permute-start.13 = (f32[80,128]{1,0:T(8,128)S(1)}, f32[80,128]{1,0:T(8,128)S(1)}, u32[]{:S(2)}, u32[]{:S(2)}) collective-permute-start(f32[80,128]{1,0:T(8,128)S(1)} %get-tuple-element.61), channel_id=1, source_target_pairs={{0,7},{1,2},{2,1},{3,4},{4,3},{5,6},{6,5},{7,0},{8,15},{9,10},{10,... | collective-permute-start | bytes 122888 | tf_op jit(solution)/shard_map/ppermute | solution.py:622
  42.6 0.0 collective-permute-done.3.fxb
  42.6 1.1 %shard_map.88 = f32[27,4,16,128]{3,2,1,0:T(8,128)} custom-call(f32[27,4,16,128]{3,2,1,0:T(8,128)S(1)} %get-tuple-element.32.post, f32[9,16,128]{2,1,0:T(8,128)S(1)} %collective-permute-done.2.fxa, f32[9,16,128]{2,1,0:T(8,128)S(1)} %collective-permute-done.3.fxb, f32[116,128]{1,0:T(8,128)S(1)} %collective-permute-done.hya.refs_9_, ...), custom_call_target="tpu_custom_call" | custom-call | flops 2000000 | bytes 2000000 | tf_op jit(solution)/shard_map/pallas_call | solution.py:64
  43.7 2.0 %shard_map.93.refs_0_ = f32[7,20,4,16,128]{4,3,2,1,0:T(8,128)S(1)} custom-call(f32[7,20,4,16,128]{4,3,2,1,0:T(8,128)S(1)} %shard_map.91.g.refs_0_, f32[7,20,4,16,128]{4,3,2,1,0:T(8,128)S(1)} %get-tuple-element.55.refs_1_, f32[20,40,128]{2,1,0:T(8,128)S(1)} %get-tuple-element.56.refs_2_, ...), custom_call_target="tpu_custom_call", output_to_operand_aliasing={{}: (1, {})} | custom-call | flops 2000000 | bytes 2000000 | tf_op jit(solution)/shard_map/pallas_call | solution.py:64
  45.7 1.9 %shard_map.94.refs_5_ = f32[7,20,4,16,128]{4,3,2,1,0:T(8,128)} custom-call(f32[7,20,4,16,128]{4,3,2,1,0:T(8,128)S(1)} %shard_map.93.refs_0_, s32[4,16,128]{2,1,0:T(8,128)S(1)} %copy-done, f32[11,20,128]{2,1,0:T(8,128)S(1)} %get-tuple-element.47.fixed.refs_12_.refs_2_.refs_4_), custom_call_target="tpu_custom_call" | custom-call | flops 2000000 | bytes 2000000 | tf_op jit(solution)/shard_map/pallas_call | solution.py:64
  47.6 0.0 collective-permute-done.12.refs_1_
  47.6 1.4 %shard_map.95.refs_5_ = f32[7,20,4,16,128]{4,3,2,1,0:T(8,128)} custom-call(f32[7,20,4,16,128]{4,3,2,1,0:T(8,128)S(1)} %shard_map.93.refs_0_, f32[80,128]{1,0:T(8,128)S(1)} %collective-permute-done.12.refs_1_, f32[80,128]{1,0:T(8,128)S(1)} %collective-permute-done.13.refs_2_, s32[4,16,128]{2,1,0:T(8,128)S(1)} %copy-done, ...), custom_call_target="tpu_custom_call", output_to_operand_aliasing={{}: (5, {})} | custom-call | flops 2000000 | bytes 2000000 | tf_op jit(solution)/shard_map/pallas_call | solution.py:64
  49.1 1.1 %shard_map.96 = f32[7,20,4,16,128]{4,3,2,1,0:T(8,128)} custom-call(f32[7,20,4,16,128]{4,3,2,1,0:T(8,128)S(1)} %shard_map.93.refs_0_, f32[20,16,128]{2,1,0:T(8,128)S(1)} %collective-permute-done.10.refs_1_, f32[20,16,128]{2,1,0:T(8,128)S(1)} %collective-permute-done.11.refs_2_, s32[4,16,128]{2,1,0:T(8,128)S(1)} %copy-done, ...), custom_call_target="tpu_custom_call", output_to_operand_aliasing={{}: (5, {})} | custom-call | flops 2000000 | bytes 2000000 | tf_op jit(solution)/shard_map/pallas_call | solution.py:64
  (9 shorter events, 0.0 us)
Async XLA Ops:
  4.5 9.8 %collective-permute-start.4 = (f32[20,16,128]{2,1,0:T(8,128)S(1)}, f32[20,16,128]{2,1,0:T(8,128)S(1)}, u32[]{:S(2)}, u32[]{:S(2)}) collective-permute-start(f32[20,16,128]{2,1,0:T(8,128)S(1)} %get-tuple-element.45), channel_id=1, source_target_pairs={{0,8},{8,0},{16,24},{24,16},{1,9},{9,1},{17,25},{25,17},{2,10},{10... | collective-permute-start | bytes 491528 | tf_op jit(solution)/shard_map/ppermute | solution.py:623
  6.7 9.4 %collective-permute-start.5 = (f32[20,16,128]{2,1,0:T(8,128)S(1)}, f32[20,16,128]{2,1,0:T(8,128)S(1)}, u32[]{:S(2)}, u32[]{:S(2)}) collective-permute-start(f32[20,16,128]{2,1,0:T(8,128)S(1)} %get-tuple-element.46), channel_id=1, source_target_pairs={{0,24},{8,16},{16,8},{24,0},{1,25},{9,17},{17,9},{25,1},{2,26},{10... | collective-permute-start | bytes 491528 | tf_op jit(solution)/shard_map/ppermute | solution.py:622
  8.9 4.0 %collective-permute-start = (f32[116,128]{1,0:T(8,128)S(1)}, f32[116,128]{1,0:T(8,128)S(1)}, u32[]{:S(2)}, u32[]{:S(2)}) collective-permute-start(f32[116,128]{1,0:T(8,128)S(1)} %get-tuple-element.33), channel_id=1, source_target_pairs={{0,1},{1,0},{2,3},{3,2},{4,5},{5,4},{6,7},{7,6},{8,9},{9,8},{10,11... | collective-permute-start | bytes 178184 | tf_op jit(solution)/shard_map/ppermute | solution.py:623
  10.1 4.2 %collective-permute-start.1 = (f32[116,128]{1,0:T(8,128)S(1)}, f32[116,128]{1,0:T(8,128)S(1)}, u32[]{:S(2)}, u32[]{:S(2)}) collective-permute-start(f32[116,128]{1,0:T(8,128)S(1)} %get-tuple-element.34), channel_id=1, source_target_pairs={{0,7},{1,2},{2,1},{3,4},{4,3},{5,6},{6,5},{7,0},{8,15},{9,10},{10,... | collective-permute-start | bytes 178184 | tf_op jit(solution)/shard_map/ppermute | solution.py:622
  11.2 4.8 %copy-start = (s32[4,16,128]{2,1,0:T(8,128)S(1)}, s32[4,16,128]{2,1,0:T(8,128)}, u32[]{:S(2)}) copy-start(s32[4,16,128]{2,1,0:T(8,128)} %refs_3_.3) | copy-start | bytes 98308
  17.8 8.8 %collective-permute-start.6 = (f32[20,16,128]{2,1,0:T(8,128)S(1)}, f32[20,16,128]{2,1,0:T(8,128)S(1)}, u32[]{:S(2)}, u32[]{:S(2)}) collective-permute-start(f32[20,16,128]{2,1,0:T(8,128)S(1)} %get-tuple-element.51), channel_id=1, source_target_pairs={{0,8},{8,0},{16,24},{24,16},{1,9},{9,1},{17,25},{25,17},{2,10},{10... | collective-permute-start | bytes 491528 | tf_op jit(solution)/shard_map/ppermute | solution.py:623
  17.9 8.7 %collective-permute-start.7 = (f32[20,16,128]{2,1,0:T(8,128)S(1)}, f32[20,16,128]{2,1,0:T(8,128)S(1)}, u32[]{:S(2)}, u32[]{:S(2)}) collective-permute-start(f32[20,16,128]{2,1,0:T(8,128)S(1)} %get-tuple-element.52), channel_id=1, source_target_pairs={{0,24},{8,16},{16,8},{24,0},{1,25},{9,17},{17,9},{25,1},{2,26},{10... | collective-permute-start | bytes 491528 | tf_op jit(solution)/shard_map/ppermute | solution.py:622
  20.5 5.2 %collective-permute-start.8 = (f32[80,128]{1,0:T(8,128)S(1)}, f32[80,128]{1,0:T(8,128)S(1)}, u32[]{:S(2)}, u32[]{:S(2)}) collective-permute-start(f32[80,128]{1,0:T(8,128)S(1)} %get-tuple-element.53), channel_id=1, source_target_pairs={{0,1},{1,0},{2,3},{3,2},{4,5},{5,4},{6,7},{7,6},{8,9},{9,8},{10,11... | collective-permute-start | bytes 122888 | tf_op jit(solution)/shard_map/ppermute | solution.py:623
  22.6 3.9 %collective-permute-start.9 = (f32[80,128]{1,0:T(8,128)S(1)}, f32[80,128]{1,0:T(8,128)S(1)}, u32[]{:S(2)}, u32[]{:S(2)}) collective-permute-start(f32[80,128]{1,0:T(8,128)S(1)} %get-tuple-element.54), channel_id=1, source_target_pairs={{0,7},{1,2},{2,1},{3,4},{4,3},{5,6},{6,5},{7,0},{8,15},{9,10},{10,... | collective-permute-start | bytes 122888 | tf_op jit(solution)/shard_map/ppermute | solution.py:622
  28.2 20.8 %collective-permute-start.10 = (f32[20,16,128]{2,1,0:T(8,128)S(1)}, f32[20,16,128]{2,1,0:T(8,128)S(1)}, u32[]{:S(2)}, u32[]{:S(2)}) collective-permute-start(f32[20,16,128]{2,1,0:T(8,128)S(1)} %get-tuple-element.58), channel_id=1, source_target_pairs={{0,8},{8,0},{16,24},{24,16},{1,9},{9,1},{17,25},{25,17},{2,10},{10... | collective-permute-start | bytes 491528 | tf_op jit(solution)/shard_map/ppermute | solution.py:623
  28.3 20.7 %collective-permute-start.11 = (f32[20,16,128]{2,1,0:T(8,128)S(1)}, f32[20,16,128]{2,1,0:T(8,128)S(1)}, u32[]{:S(2)}, u32[]{:S(2)}) collective-permute-start(f32[20,16,128]{2,1,0:T(8,128)S(1)} %get-tuple-element.59), channel_id=1, source_target_pairs={{0,24},{8,16},{16,8},{24,0},{1,25},{9,17},{17,9},{25,1},{2,26},{10... | collective-permute-start | bytes 491528 | tf_op jit(solution)/shard_map/ppermute | solution.py:622
  30.4 5.9 %collective-permute-start.2 = (f32[9,16,128]{2,1,0:T(8,128)S(1)}, f32[9,16,128]{2,1,0:T(8,128)S(1)}, u32[]{:S(2)}, u32[]{:S(2)}) collective-permute-start(f32[9,16,128]{2,1,0:T(8,128)S(1)} %get-tuple-element.35), channel_id=1, source_target_pairs={{0,8},{8,0},{16,24},{24,16},{1,9},{9,1},{17,25},{25,17},{2,10},{10... | collective-permute-start | bytes 221192 | tf_op jit(solution)/shard_map/ppermute | solution.py:623
  30.9 11.7 %collective-permute-start.3 = (f32[9,16,128]{2,1,0:T(8,128)S(1)}, f32[9,16,128]{2,1,0:T(8,128)S(1)}, u32[]{:S(2)}, u32[]{:S(2)}) collective-permute-start(f32[9,16,128]{2,1,0:T(8,128)S(1)} %get-tuple-element.36), channel_id=1, source_target_pairs={{0,24},{8,16},{16,8},{24,0},{1,25},{9,17},{17,9},{25,1},{2,26},{10... | collective-permute-start | bytes 221192 | tf_op jit(solution)/shard_map/ppermute | solution.py:622
  32.2 15.4 %collective-permute-start.12 = (f32[80,128]{1,0:T(8,128)S(1)}, f32[80,128]{1,0:T(8,128)S(1)}, u32[]{:S(2)}, u32[]{:S(2)}) collective-permute-start(f32[80,128]{1,0:T(8,128)S(1)} %get-tuple-element.60), channel_id=1, source_target_pairs={{0,1},{1,0},{2,3},{3,2},{4,5},{5,4},{6,7},{7,6},{8,9},{9,8},{10,11... | collective-permute-start | bytes 122888 | tf_op jit(solution)/shard_map/ppermute | solution.py:623
  36.3 11.4 %collective-permute-start.13 = (f32[80,128]{1,0:T(8,128)S(1)}, f32[80,128]{1,0:T(8,128)S(1)}, u32[]{:S(2)}, u32[]{:S(2)}) collective-permute-start(f32[80,128]{1,0:T(8,128)S(1)} %get-tuple-element.61), channel_id=1, source_target_pairs={{0,7},{1,2},{2,1},{3,4},{4,3},{5,6},{6,5},{7,0},{8,15},{9,10},{10,... | collective-permute-start | bytes 122888 | tf_op jit(solution)/shard_map/ppermute | solution.py:622
where the time goes:
time: 50.4 us; the launch traced here: 50.2 us
  starting transfers between devices  26.8 us (53%)
  Pallas kernels  18.4 us (37%)
  waiting for transfers between devices  4.21 us (8%)
  between operations  0.78 us (2%)
    pallas_call x11, Pallas kernels, call(): pl.pallas_call(body, out_shape=outs, in_specs=specs, out_specs=out_specs,...  18.4 us
    ppermute x7, starting transfers between devices, swap(): far = lax.ppermute(far, axis, pairs(size, False))  16.7 us
    ppermute x7, starting transfers between devices, swap(): near = lax.ppermute(near, axis, pairs(size, True))  10.1 us
    ppermute x7, waiting for transfers between devices, swap(): far = lax.ppermute(far, axis, pairs(size, False))  3.99 us
  transfers between devices with their start and end apart: 14, of which 4 were waited for; matrix products, arithmetic and copies ran while one was open for 0% of the time, Pallas kernels for 20%

commit v1 on v0

--- a/solution.py
+++ b/solution.py
@@ -9,7 +9,7 @@
 
 
 SUBSTEPS = 3
-CONC = 10
+CONC = 20
 OMEGA = 1.6
 SPEED = 0.05
 F32 = jnp.float32
@@ -79,21 +79,19 @@
     tiles = (part.stop - part.start) // 8
     half = w_ref.shape[1] // 2
     even = tiles - tiles % 2
-    for i in range(half // 16):
-        rates = []
-        for n in range(2):
-            j = 2 * i + n
-            rates.append(c_ref[rx[0, j], part, :] * (c_ref[rx[1, j], part, :] * kc[j]))
-        for t in range(tiles):
-            both = jnp.concatenate([r[8 * t : 8 * t + 8] for r in rates], axis=0)
+    for j in range(half // 8):
+        rate = c_ref[rx[0, j], part, :] * (c_ref[rx[1, j], part, :] * kc[j])
+        at = slice(8 * j, 8 * j + 8)
+        for t in range(0, even, 2):
+            both = jnp.concatenate([rate[8 * t : 8 * t + 8], rate[8 * t + 8 : 8 * t + 16]], axis=1)
             high = both.astype(BF16)
             low = (both - high.astype(F32)).astype(BF16)
-            if t < even:
-                rt_ref[16 * i : 16 * i + 16, lanes * t : lanes * (t + 1)] = high
-                rt_ref[half + 16 * i : half + 16 * i + 16, lanes * t : lanes * (t + 1)] = low
-            else:
-                odd_ref[16 * i : 16 * i + 16, :lanes] = high
-                odd_ref[16 * i : 16 * i + 16, lanes:] = low
+            rt_ref[at, lanes * t : lanes * (t + 2)] = high
+            rt_ref[half + 8 * j : half + 8 * j + 8, lanes * t : lanes * (t + 2)] = low
+        if even < tiles:
+            last = rate[8 * even :]
+            rest = last - last.astype(BF16).astype(F32)
+            odd_ref[at, :] = jnp.concatenate([last, rest], axis=1).astype(BF16)
     if even < tiles:
         total = jnp.dot(w_ref[:, :half], odd_ref[...], preferred_element_type=F32)
         total = total[:, :lanes] + total[:, lanes:]
@@ -424,14 +422,16 @@
     send_rows(new, keep, c03, s03, fixed, u, ya, yb)
 
 
-def rest_body(moving, *refs):
+def rest_body(moving, final, *refs):
     refs = list(refs)
     g = refs.pop(0) if moving else None
     start, c03, s03, u, rx, kc, rk, w = [refs.pop(0) for _ in range(8)]
     if moving:
         hya, hyb, nt, fixed = [refs.pop(0) for _ in range(4)]
         hy = Halo(hya, hyb, "gy")
-    new, c12, s12, rt = refs
+    new = refs.pop(0)
+    result = refs.pop(0) if final else None
+    c12, s12, rt = refs[:3]
     species, planes, rows, _ = new.shape[1:]
     for x in range(1, planes - 1):
         kind = masks(nt, x) if moving else None
@@ -454,28 +454,65 @@
 
         lax.fori_loop(0, species, step, 0, unroll=CONC)
     react(rx, kc, c12, s12, w, rt)
+    chunk = 5 if final and species % 5 == 0 else species
+    copies = []
+    for begin in range(0, species, chunk):
+        end = begin + chunk
+        for x in range(planes):
+            ux, uy, uz = 0.5 * u[0, x], 0.5 * u[1, x], 0.5 * u[2, x]
+            if x in (0, planes - 1):
+                cr, sr, half = c03, s03, slice((x > 0) * rows, (x > 0) * rows + rows)
+            else:
+                cr, sr, half = c12, s12, slice((x - 1) * rows, x * rows)
+
+            def collide(k, carry, x=x, cr=cr, sr=sr, half=half, ux=ux, uy=uy, uz=uz):
+                r = rk[k]
+                keep = 1.0 - r
+                a = r * cr[k, half, :]
+                base1 = 0.125 * (a + sr[k, half, :])
+                new[0, k, x] = keep * new[0, k, x] + (base1 + base1)
+                for i, v in ((1, ux), (3, uy), (5, uz)):
+                    d = a * v
+                    up = keep * new[i, k, x] + (base1 + d)
+                    down = keep * new[i + 1, k, x] + (base1 - d)
+                    new[i, k, x] = up
+                    new[i + 1, k, x] = down
+                return carry
+
+            lax.fori_loop(begin, end, collide, 0, unroll=5)
+        if final:
+            copies += put_out(
+                {0: range(planes), 5: range(planes), 1: range(1, planes - 1)},
+                slice(begin, end), new, None, None, nt, fixed, result, refs[3], refs[4], len(copies),
+            )
+    for copy in copies:
+        copy.wait()
+
+
+def put_out(cover, part, g, hx, hy, nt, fixed, result, buf, sem, used):
+    planes = g.shape[2]
     for x in range(planes):
-        ux, uy, uz = 0.5 * u[0, x], 0.5 * u[1, x], 0.5 * u[2, x]
-        if x in (0, planes - 1):
-            cr, sr, half = c03, s03, slice((x > 0) * rows, (x > 0) * rows + rows)
-        else:
-            cr, sr, half = c12, s12, slice((x - 1) * rows, x * rows)
-
-        def collide(k, carry, x=x, cr=cr, sr=sr, half=half, ux=ux, uy=uy, uz=uz):
-            r = rk[k]
-            keep = 1.0 - r
-            a = r * cr[k, half, :]
-            base1 = 0.125 * (a + sr[k, half, :])
-            new[0, k, x] = keep * new[0, k, x] + (base1 + base1)
-            for i, v in ((1, ux), (3, uy), (5, uz)):
-                d = a * v
-                up = keep * new[i, k, x] + (base1 + d)
-                down = keep * new[i + 1, k, x] + (base1 - d)
-                new[i, k, x] = up
-                new[i + 1, k, x] = down
-            return carry
-
-        lax.fori_loop(0, species, collide, 0, unroll=5)
+        pairs = [p for p, xs in cover.items() if x in xs]
+        kind = masks(nt, x)
+        for k in range(part.start, part.stop):
+            values = walled(gather(k, x, g, hx, hy, pairs), kind, k, fixed)
+            for i, value in values.items():
+                buf[i, k, x] = value
+    copies = []
+    for pair, xs in cover.items():
+        for i in (0,) if pair == 0 else (pair, pair + 1):
+            if len(xs) == planes or 0 not in xs:
+                spans = [slice(xs[0], xs[-1] + 1)]
+            else:
+                spans = [slice(x, x + 1) for x in xs]
+            for span in spans:
+                at = (i, part, span)
+                copies.append(
+                    pltpu.make_async_copy(buf.at[at], result.at[at], sem.at[used + len(copies)])
+                )
+    for copy in copies:
+        copy.start()
+    return copies
 
 
 def faces_body(species, post, hya, hyb, fa, fb):
@@ -540,54 +577,17 @@
         copy.wait()
 
 
-def end_body(mode, *refs):
-    refs = list(refs)
-    g = refs.pop(0)
-    hx = Halo(refs.pop(0), refs.pop(0), "gx") if mode == 1 else None
-    hy = Halo(refs.pop(0), refs.pop(0), "gy") if mode == 3 else None
-    nt, fixed = [refs.pop(0) for _ in range(2)]
-    if mode:
-        refs.pop(0)
-    out, buf, sem = refs
+def end_body(g, hxa, hxb, hya, hyb, nt, fixed, before, out, buf, sem):
+    del before
     species, planes = g.shape[1:3]
-    inner = range(1, planes - 1)
-    cover = {
-        0: {0: range(planes), 5: range(planes), 1: inner},
-        3: {3: range(planes)},
-        1: {1: (0, planes - 1)},
-    }[mode]
-    chunk = 5 if species % 5 == 0 else 1
+    hx, hy = Halo(hxa, hxb, "gx"), Halo(hya, hyb, "gy")
+    chunk = 5 if species % 5 == 0 else species
     copies = []
-    for start in range(0, species, chunk):
-        for x in range(planes):
-            pairs = [p for p, xs in cover.items() if x in xs]
-            if not pairs:
-                continue
-            kind = masks(nt, x)
-
-            def step(k, carry, x=x, pairs=pairs, kind=kind):
-                values = walled(gather(k, x, g, hx, hy, pairs), kind, k, fixed)
-                for i, value in values.items():
-                    buf[i - mode, k, x] = value
-                return carry
-
-            lax.fori_loop(start, start + chunk, step, 0, unroll=True)
-        part = slice(start, start + chunk)
-        for pair in cover:
-            for i in (0,) if pair == 0 else (pair, pair + 1):
-                if pair != 1:
-                    spans = [slice(0, planes)]
-                elif mode == 0:
-                    spans = [slice(1, planes - 1)]
-                else:
-                    spans = [slice(0, 1), slice(planes - 1, planes)]
-                for span in spans:
-                    copies.append(
-                        pltpu.make_async_copy(
-                            buf.at[i - mode, part, span], out.at[i, part, span], sem.at[len(copies)]
-                        )
-                    )
-                    copies[-1].start()
+    for begin in range(0, species, chunk):
+        copies += put_out(
+            {3: range(planes), 1: (0, planes - 1)},
+            slice(begin, begin + chunk), g, hx, hy, nt, fixed, out, buf, sem, len(copies),
+        )
     for copy in copies:
         copy.wait()
 
@@ -667,13 +667,15 @@
         if moving:
             ins += [inv(v) for v in (*halo, node_type, fixed)]
         specs += [VM] * (len(ins) - len(specs))
-        (g,) = call(
-            functools.partial(rest_body, moving),
+        final = s == SUBSTEPS - 1
+        shape = pltpu.HBM((7, count, planes, rows, lanes), F32)
+        g, *result = call(
+            functools.partial(rest_body, moving, final),
             ins,
             specs,
-            (state,),
-            [VM],
-            [inside, inside, rates_in],
+            (state, shape) if final else (state,),
+            [VM, ANY] if final else [VM],
+            [inside, inside, rates_in] + ([state, pltpu.SemaphoreType.DMA((32,))] if final else []),
             alias={1 if moving else 0: 0},
         )
         if not moving:
@@ -694,20 +696,16 @@
         ANY,
         [flows, sems[0]],
     )
-    result = None
-    for mode, extra in ((0, ()), (3, hy), (1, hx)):
-        ins = [inv(v) for v in (g,) + extra] + [nt, inv(fixed)] + ([hbm(result)] if mode else [])
-        result = call(
-            functools.partial(end_body, mode),
-            ins,
-            [VM] * (3 + len(extra)) + ([ANY] if mode else []),
-            pltpu.HBM((7, count, planes, rows, lanes), F32),
-            ANY,
-            [VMEM((7 if mode == 0 else 2, count, planes, rows, lanes), F32),
-             pltpu.SemaphoreType.DMA((32,))],
-            alias={len(ins) - 1: 0} if mode else None,
-        )
-    return new_populations, result
+    new_species = call(
+        end_body,
+        [inv(v) for v in (g, *hx, *hy, node_type, fixed)] + [hbm(result[0])],
+        [VM] * 7 + [ANY],
+        shape,
+        ANY,
+        [state, pltpu.SemaphoreType.DMA((32,))],
+        alias={7: 0},
+    )
+    return new_populations, new_species
 
 
 def solution(mesh):

time: 50.4 us -> 48.8 us (0.968)
  Pallas kernels: 18.4 us -> 16.6 us
    pallas_call x11 -> x9, Pallas kernels: 18.4 us -> 16.6 us  [call(): pl.pallas_call(body, out_shape=outs, in_specs=specs, out_specs=out_specs,...]
  transfers between devices with their start and end apart: 14 -> 14, of which waited for: 4 -> 4; matrix products, arithmetic and copies ran while one was open for 0% -> 0% of each run, Pallas kernels for 20% -> 17%
where the time goes in v1:
time: 48.8 us; the launch traced here: 48.6 us
  starting transfers between devices  26.8 us (55%)
  Pallas kernels  16.6 us (34%)
  waiting for transfers between devices  4.41 us (9%)
  between operations  0.76 us (2%)
    ppermute x7, starting transfers between devices, swap(): far = lax.ppermute(far, axis, pairs(size, False))  16.7 us
    pallas_call x9, Pallas kernels, call(): pl.pallas_call(body, out_shape=outs, in_specs=specs, out_specs=out_specs,...  16.6 us
    ppermute x7, starting transfers between devices, swap(): near = lax.ppermute(near, axis, pairs(size, True))  10.1 us
    ppermute x7, waiting for transfers between devices, swap(): far = lax.ppermute(far, axis, pairs(size, False))  4.19 us
  transfers between devices with their start and end apart: 14, of which 4 were waited for; matrix products, arithmetic and copies ran while one was open for 0% of the time, Pallas kernels for 17%

profile of v1, /device:TPU:1, one launch (start us, length us, event | category | flops | bytes accessed | tf_op | source)
XLA Modules:
  0.0 48.6 jit_solution(9806560899675782253)
XLA Ops:
  0.6 3.8 %shard_map.86 = (f32[7,20,4,16,128]{4,3,2,1,0:T(8,128)S(1)}, bf16[160,1344]{1,0:T(8,128)(2,1)S(1)}, f32[20,16,128]{2,1,0:T(8,128)S(1)}, f32[20,16,128]{2,1,0:T(8...) custom-call(f32[27,4,16,128]{3,2,1,0:T(8,128)} %pop.1, ...), custom_call_target="tpu_custom_call" | custom-call | flops 2000000 | bytes 2000000 | tf_op jit(solution)/shard_map/pallas_call | solution.py:64
  4.4 2.2 %collective-permute-start.4 = (f32[20,16,128]{2,1,0:T(8,128)S(1)}, f32[20,16,128]{2,1,0:T(8,128)S(1)}, u32[]{:S(2)}, u32[]{:S(2)}) collective-permute-start(f32[20,16,128]{2,1,0:T(8,128)S(1)} %get-tuple-element.47), channel_id=1, source_target_pairs={{0,8},{8,0},{16,24},{24,16},{1,9},{9,1},{17,25},{25,17},{2,10},{10... | collective-permute-start | bytes 491528 | tf_op jit(solution)/shard_map/ppermute | solution.py:623
  6.6 2.2 %collective-permute-start.5 = (f32[20,16,128]{2,1,0:T(8,128)S(1)}, f32[20,16,128]{2,1,0:T(8,128)S(1)}, u32[]{:S(2)}, u32[]{:S(2)}) collective-permute-start(f32[20,16,128]{2,1,0:T(8,128)S(1)} %get-tuple-element.48), channel_id=1, source_target_pairs={{0,24},{8,16},{16,8},{24,0},{1,25},{9,17},{17,9},{25,1},{2,26},{10... | collective-permute-start | bytes 491528 | tf_op jit(solution)/shard_map/ppermute | solution.py:622
  8.8 1.2 %collective-permute-start = (f32[116,128]{1,0:T(8,128)S(1)}, f32[116,128]{1,0:T(8,128)S(1)}, u32[]{:S(2)}, u32[]{:S(2)}) collective-permute-start(f32[116,128]{1,0:T(8,128)S(1)} %get-tuple-element.35), channel_id=1, source_target_pairs={{0,1},{1,0},{2,3},{3,2},{4,5},{5,4},{6,7},{7,6},{8,9},{9,8},{10,11... | collective-permute-start | bytes 178184 | tf_op jit(solution)/shard_map/ppermute | solution.py:623
  10.0 1.1 %collective-permute-start.1 = (f32[116,128]{1,0:T(8,128)S(1)}, f32[116,128]{1,0:T(8,128)S(1)}, u32[]{:S(2)}, u32[]{:S(2)}) collective-permute-start(f32[116,128]{1,0:T(8,128)S(1)} %get-tuple-element.36), channel_id=1, source_target_pairs={{0,7},{1,2},{2,1},{3,4},{4,3},{5,6},{6,5},{7,0},{8,15},{9,10},{10,... | collective-permute-start | bytes 178184 | tf_op jit(solution)/shard_map/ppermute | solution.py:622
  11.1 1.6 %shard_map.89.g.refs_0_ = f32[7,20,4,16,128]{4,3,2,1,0:T(8,128)S(1)} custom-call(f32[7,20,4,16,128]{4,3,2,1,0:T(8,128)S(1)} %get-tuple-element.39.refs_0_, f32[20,40,128]{2,1,0:T(8,128)S(1)} %get-tuple-element.40.refs_1_, f32[20,40,128]{2,1,0:T(8,128)S(1)} %get-tuple-element.41.refs_2_, ...), custom_call_target="tpu_custom_call", output_to_operand_aliasing={{}: (0, {})} | custom-call | flops 2000000 | bytes 2000000 | tf_op jit(solution)/shard_map/pallas_call | solution.py:64
  12.7 1.5 %collective-permute-done.1.hyb.refs_10_ = f32[116,128]{1,0:T(8,128)S(1)} collective-permute-done((f32[116,128]{1,0:T(8,128)S(1)}, f32[116,128]{1,0:T(8,128)S(1)}, u32[]{:S(2)}, u32[]{:S(2)}) %collective-permute-start.1) | collective-permute-done | bytes 59424 | tf_op jit(solution)/shard_map/ppermute | solution.py:622
  14.2 1.8 %collective-permute-done.5.hxb = f32[20,16,128]{2,1,0:T(8,128)S(1)} collective-permute-done((f32[20,16,128]{2,1,0:T(8,128)S(1)}, f32[20,16,128]{2,1,0:T(8,128)S(1)}, u32[]{:S(2)}, u32[]{:S(2)}) %collective-permute-start.5) | collective-permute-done | bytes 163872 | tf_op jit(solution)/shard_map/ppermute | solution.py:622
  15.9 1.6 %shard_map.90 = (f32[7,20,4,16,128]{4,3,2,1,0:T(8,128)S(1)}, f32[20,16,128]{2,1,0:T(8,128)S(1)}, f32[20,16,128]{2,1,0:T(8,128)S(1)}, f32[80,128]{1,0:T(8,128)S(1...) custom-call(f32[7,20,4,16,128]{4,3,2,1,0:T(8,128)S(1)} %shard_map.89.g.refs_0_, ...), custom_call_target="tpu_custom_call" | custom-call | flops 2000000 | bytes 2000000 | tf_op jit(solution)/shard_map/pallas_call | solution.py:64
  17.5 0.1 collective-permute-start.6
  17.6 2.6 %collective-permute-start.7 = (f32[20,16,128]{2,1,0:T(8,128)S(1)}, f32[20,16,128]{2,1,0:T(8,128)S(1)}, u32[]{:S(2)}, u32[]{:S(2)}) collective-permute-start(f32[20,16,128]{2,1,0:T(8,128)S(1)} %get-tuple-element.54), channel_id=1, source_target_pairs={{0,24},{8,16},{16,8},{24,0},{1,25},{9,17},{17,9},{25,1},{2,26},{10... | collective-permute-start | bytes 491528 | tf_op jit(solution)/shard_map/ppermute | solution.py:622
  20.3 2.2 %collective-permute-start.8 = (f32[80,128]{1,0:T(8,128)S(1)}, f32[80,128]{1,0:T(8,128)S(1)}, u32[]{:S(2)}, u32[]{:S(2)}) collective-permute-start(f32[80,128]{1,0:T(8,128)S(1)} %get-tuple-element.55), channel_id=1, source_target_pairs={{0,1},{1,0},{2,3},{3,2},{4,5},{5,4},{6,7},{7,6},{8,9},{9,8},{10,11... | collective-permute-start | bytes 122888 | tf_op jit(solution)/shard_map/ppermute | solution.py:623
  22.4 1.1 %collective-permute-start.9 = (f32[80,128]{1,0:T(8,128)S(1)}, f32[80,128]{1,0:T(8,128)S(1)}, u32[]{:S(2)}, u32[]{:S(2)}) collective-permute-start(f32[80,128]{1,0:T(8,128)S(1)} %get-tuple-element.56), channel_id=1, source_target_pairs={{0,7},{1,2},{2,1},{3,4},{4,3},{5,6},{6,5},{7,0},{8,15},{9,10},{10,... | collective-permute-start | bytes 122888 | tf_op jit(solution)/shard_map/ppermute | solution.py:622
  23.5 1.8 %shard_map.91.g.refs_0_ = f32[7,20,4,16,128]{4,3,2,1,0:T(8,128)S(1)} custom-call(f32[7,20,4,16,128]{4,3,2,1,0:T(8,128)S(1)} %shard_map.89.g.refs_0_, f32[7,20,4,16,128]{4,3,2,1,0:T(8,128)S(1)} %get-tuple-element.50.refs_1_, f32[20,40,128]{2,1,0:T(8,128)S(1)} %get-tuple-element.51.refs_2_, ...), custom_call_target="tpu_custom_call", output_to_operand_aliasing={{}: (1, {})} | custom-call | flops 2000000 | bytes 2000000 | tf_op jit(solution)/shard_map/pallas_call | solution.py:64
  25.4 0.9 %collective-permute-done.9.hyb.refs_10_ = f32[80,128]{1,0:T(8,128)S(1)} collective-permute-done((f32[80,128]{1,0:T(8,128)S(1)}, f32[80,128]{1,0:T(8,128)S(1)}, u32[]{:S(2)}, u32[]{:S(2)}) %collective-permute-start.9) | collective-permute-done | bytes 40992 | tf_op jit(solution)/shard_map/ppermute | solution.py:622
  26.3 0.0 collective-permute-done.6.hxa
  26.3 0.0 collective-permute-done.7.hxb
  26.3 1.6 %shard_map.92 = (f32[7,20,4,16,128]{4,3,2,1,0:T(8,128)S(1)}, f32[20,16,128]{2,1,0:T(8,128)S(1)}, f32[20,16,128]{2,1,0:T(8,128)S(1)}, f32[80,128]{1,0:T(8,128)S(1...) custom-call(f32[7,20,4,16,128]{4,3,2,1,0:T(8,128)S(1)} %shard_map.91.g.refs_0_, ...), custom_call_target="tpu_custom_call" | custom-call | flops 2000000 | bytes 2000000 | tf_op jit(solution)/shard_map/pallas_call | solution.py:64
  27.9 0.1 collective-permute-start.10
  28.0 2.0 %collective-permute-start.11 = (f32[20,16,128]{2,1,0:T(8,128)S(1)}, f32[20,16,128]{2,1,0:T(8,128)S(1)}, u32[]{:S(2)}, u32[]{:S(2)}) collective-permute-start(f32[20,16,128]{2,1,0:T(8,128)S(1)} %get-tuple-element.62), channel_id=1, source_target_pairs={{0,24},{8,16},{16,8},{24,0},{1,25},{9,17},{17,9},{25,1},{2,26},{10... | collective-permute-start | bytes 491528 | tf_op jit(solution)/shard_map/ppermute | solution.py:622
  30.1 0.6 %collective-permute-start.2 = (f32[9,16,128]{2,1,0:T(8,128)S(1)}, f32[9,16,128]{2,1,0:T(8,128)S(1)}, u32[]{:S(2)}, u32[]{:S(2)}) collective-permute-start(f32[9,16,128]{2,1,0:T(8,128)S(1)} %get-tuple-element.37), channel_id=1, source_target_pairs={{0,8},{8,0},{16,24},{24,16},{1,9},{9,1},{17,25},{25,17},{2,10},{10... | collective-permute-start | bytes 221192 | tf_op jit(solution)/shard_map/ppermute | solution.py:623
  30.6 1.3 %collective-permute-start.3 = (f32[9,16,128]{2,1,0:T(8,128)S(1)}, f32[9,16,128]{2,1,0:T(8,128)S(1)}, u32[]{:S(2)}, u32[]{:S(2)}) collective-permute-start(f32[9,16,128]{2,1,0:T(8,128)S(1)} %get-tuple-element.38), channel_id=1, source_target_pairs={{0,24},{8,16},{16,8},{24,0},{1,25},{9,17},{17,9},{25,1},{2,26},{10... | collective-permute-start | bytes 221192 | tf_op jit(solution)/shard_map/ppermute | solution.py:622
  31.9 3.8 %collective-permute-start.12 = (f32[80,128]{1,0:T(8,128)S(1)}, f32[80,128]{1,0:T(8,128)S(1)}, u32[]{:S(2)}, u32[]{:S(2)}) collective-permute-start(f32[80,128]{1,0:T(8,128)S(1)} %get-tuple-element.63), channel_id=1, source_target_pairs={{0,1},{1,0},{2,3},{3,2},{4,5},{5,4},{6,7},{7,6},{8,9},{9,8},{10,11... | collective-permute-start | bytes 122888 | tf_op jit(solution)/shard_map/ppermute | solution.py:623
  35.8 0.2 collective-permute-done.2.fxa
  36.0 6.4 %collective-permute-start.13 = (f32[80,128]{1,0:T(8,128)S(1)}, f32[80,128]{1,0:T(8,128)S(1)}, u32[]{:S(2)}, u32[]{:S(2)}) collective-permute-start(f32[80,128]{1,0:T(8,128)S(1)} %get-tuple-element.64), channel_id=1, source_target_pairs={{0,7},{1,2},{2,1},{3,4},{4,3},{5,6},{6,5},{7,0},{8,15},{9,10},{10,... | collective-permute-start | bytes 122888 | tf_op jit(solution)/shard_map/ppermute | solution.py:622
  42.3 0.0 collective-permute-done.3.fxb
  42.3 1.1 %shard_map.88 = f32[27,4,16,128]{3,2,1,0:T(8,128)} custom-call(f32[27,4,16,128]{3,2,1,0:T(8,128)S(1)} %get-tuple-element.34.post, f32[9,16,128]{2,1,0:T(8,128)S(1)} %collective-permute-done.2.fxa, f32[9,16,128]{2,1,0:T(8,128)S(1)} %collective-permute-done.3.fxb, f32[116,128]{1,0:T(8,128)S(1)} %collective-permute-done.hya.refs_9_, ...), custom_call_target="tpu_custom_call" | custom-call | flops 2000000 | bytes 2000000 | tf_op jit(solution)/shard_map/pallas_call | solution.py:64
  43.4 3.6 %shard_map.93 = (f32[7,20,4,16,128]{4,3,2,1,0:T(8,128)S(1)}, f32[7,20,4,16,128]{4,3,2,1,0:T(8,128)}) custom-call(f32[7,20,4,16,128]{4,3,2,1,0:T(8,128)S(1)} %shard_map.91.g.refs_0_, f32[7,20,4,16,128]{4,3,2,1,0:T(8,128)S(1)} %get-tuple-element.57.refs_1_, f32[20,40,128]{2,1,0:T(8,128)S(1)} %get-tuple-element.58.refs_2_, ...), custom_call_target="tpu_custom_call", output_to_operand_aliasing={{0}: (1, {})} | custom-call | flops 2000000 | bytes 2000000 | tf_op jit(solution)/shard_map/pallas_call | solution.py:64
  47.0 0.0 collective-permute-done.12.hya
  47.0 0.0 collective-permute-done.13.hyb
  47.0 0.0 collective-permute-done.11.hxb
  47.0 1.6 %shard_map.94 = f32[7,20,4,16,128]{4,3,2,1,0:T(8,128)} custom-call(f32[7,20,4,16,128]{4,3,2,1,0:T(8,128)S(1)} %get-tuple-element.60.g, f32[20,16,128]{2,1,0:T(8,128)S(1)} %collective-permute-done.10.hxa, f32[20,16,128]{2,1,0:T(8,128)S(1)} %collective-permute-done.11.hxb, f32[80,128]{1,0:T(8,128)S(1)} %collective-permute-done.12.hya, ...), custom_call_target="tpu_custom_call", output_to_operand_aliasing={{}: (7, {})} | custom-call | flops 2000000 | bytes 2000000 | tf_op jit(solution)/shard_map/pallas_call | solution.py:64
  (7 shorter events, 0.0 us)
Async XLA Ops:
  4.4 9.8 %collective-permute-start.4 = (f32[20,16,128]{2,1,0:T(8,128)S(1)}, f32[20,16,128]{2,1,0:T(8,128)S(1)}, u32[]{:S(2)}, u32[]{:S(2)}) collective-permute-start(f32[20,16,128]{2,1,0:T(8,128)S(1)} %get-tuple-element.47), channel_id=1, source_target_pairs={{0,8},{8,0},{16,24},{24,16},{1,9},{9,1},{17,25},{25,17},{2,10},{10... | collective-permute-start | bytes 491528 | tf_op jit(solution)/shard_map/ppermute | solution.py:623
  6.6 9.4 %collective-permute-start.5 = (f32[20,16,128]{2,1,0:T(8,128)S(1)}, f32[20,16,128]{2,1,0:T(8,128)S(1)}, u32[]{:S(2)}, u32[]{:S(2)}) collective-permute-start(f32[20,16,128]{2,1,0:T(8,128)S(1)} %get-tuple-element.48), channel_id=1, source_target_pairs={{0,24},{8,16},{16,8},{24,0},{1,25},{9,17},{17,9},{25,1},{2,26},{10... | collective-permute-start | bytes 491528 | tf_op jit(solution)/shard_map/ppermute | solution.py:622
  8.8 3.9 %collective-permute-start = (f32[116,128]{1,0:T(8,128)S(1)}, f32[116,128]{1,0:T(8,128)S(1)}, u32[]{:S(2)}, u32[]{:S(2)}) collective-permute-start(f32[116,128]{1,0:T(8,128)S(1)} %get-tuple-element.35), channel_id=1, source_target_pairs={{0,1},{1,0},{2,3},{3,2},{4,5},{5,4},{6,7},{7,6},{8,9},{9,8},{10,11... | collective-permute-start | bytes 178184 | tf_op jit(solution)/shard_map/ppermute | solution.py:623
  10.0 4.2 %collective-permute-start.1 = (f32[116,128]{1,0:T(8,128)S(1)}, f32[116,128]{1,0:T(8,128)S(1)}, u32[]{:S(2)}, u32[]{:S(2)}) collective-permute-start(f32[116,128]{1,0:T(8,128)S(1)} %get-tuple-element.36), channel_id=1, source_target_pairs={{0,7},{1,2},{2,1},{3,4},{4,3},{5,6},{6,5},{7,0},{8,15},{9,10},{10,... | collective-permute-start | bytes 178184 | tf_op jit(solution)/shard_map/ppermute | solution.py:622
  11.1 4.8 %copy-start = (s32[4,16,128]{2,1,0:T(8,128)S(1)}, s32[4,16,128]{2,1,0:T(8,128)}, u32[]{:S(2)}) copy-start(s32[4,16,128]{2,1,0:T(8,128)} %nt.7) | copy-start | bytes 98308
  17.5 8.8 %collective-permute-start.6 = (f32[20,16,128]{2,1,0:T(8,128)S(1)}, f32[20,16,128]{2,1,0:T(8,128)S(1)}, u32[]{:S(2)}, u32[]{:S(2)}) collective-permute-start(f32[20,16,128]{2,1,0:T(8,128)S(1)} %get-tuple-element.53), channel_id=1, source_target_pairs={{0,8},{8,0},{16,24},{24,16},{1,9},{9,1},{17,25},{25,17},{2,10},{10... | collective-permute-start | bytes 491528 | tf_op jit(solution)/shard_map/ppermute | solution.py:623
  17.6 8.7 %collective-permute-start.7 = (f32[20,16,128]{2,1,0:T(8,128)S(1)}, f32[20,16,128]{2,1,0:T(8,128)S(1)}, u32[]{:S(2)}, u32[]{:S(2)}) collective-permute-start(f32[20,16,128]{2,1,0:T(8,128)S(1)} %get-tuple-element.54), channel_id=1, source_target_pairs={{0,24},{8,16},{16,8},{24,0},{1,25},{9,17},{17,9},{25,1},{2,26},{10... | collective-permute-start | bytes 491528 | tf_op jit(solution)/shard_map/ppermute | solution.py:622
  20.3 5.1 %collective-permute-start.8 = (f32[80,128]{1,0:T(8,128)S(1)}, f32[80,128]{1,0:T(8,128)S(1)}, u32[]{:S(2)}, u32[]{:S(2)}) collective-permute-start(f32[80,128]{1,0:T(8,128)S(1)} %get-tuple-element.55), channel_id=1, source_target_pairs={{0,1},{1,0},{2,3},{3,2},{4,5},{5,4},{6,7},{7,6},{8,9},{9,8},{10,11... | collective-permute-start | bytes 122888 | tf_op jit(solution)/shard_map/ppermute | solution.py:623
  22.4 3.9 %collective-permute-start.9 = (f32[80,128]{1,0:T(8,128)S(1)}, f32[80,128]{1,0:T(8,128)S(1)}, u32[]{:S(2)}, u32[]{:S(2)}) collective-permute-start(f32[80,128]{1,0:T(8,128)S(1)} %get-tuple-element.56), channel_id=1, source_target_pairs={{0,7},{1,2},{2,1},{3,4},{4,3},{5,6},{6,5},{7,0},{8,15},{9,10},{10,... | collective-permute-start | bytes 122888 | tf_op jit(solution)/shard_map/ppermute | solution.py:622
  27.9 19.1 %collective-permute-start.10 = (f32[20,16,128]{2,1,0:T(8,128)S(1)}, f32[20,16,128]{2,1,0:T(8,128)S(1)}, u32[]{:S(2)}, u32[]{:S(2)}) collective-permute-start(f32[20,16,128]{2,1,0:T(8,128)S(1)} %get-tuple-element.61), channel_id=1, source_target_pairs={{0,8},{8,0},{16,24},{24,16},{1,9},{9,1},{17,25},{25,17},{2,10},{10... | collective-permute-start | bytes 491528 | tf_op jit(solution)/shard_map/ppermute | solution.py:623
  28.0 19.0 %collective-permute-start.11 = (f32[20,16,128]{2,1,0:T(8,128)S(1)}, f32[20,16,128]{2,1,0:T(8,128)S(1)}, u32[]{:S(2)}, u32[]{:S(2)}) collective-permute-start(f32[20,16,128]{2,1,0:T(8,128)S(1)} %get-tuple-element.62), channel_id=1, source_target_pairs={{0,24},{8,16},{16,8},{24,0},{1,25},{9,17},{17,9},{25,1},{2,26},{10... | collective-permute-start | bytes 491528 | tf_op jit(solution)/shard_map/ppermute | solution.py:622
  30.1 5.9 %collective-permute-start.2 = (f32[9,16,128]{2,1,0:T(8,128)S(1)}, f32[9,16,128]{2,1,0:T(8,128)S(1)}, u32[]{:S(2)}, u32[]{:S(2)}) collective-permute-start(f32[9,16,128]{2,1,0:T(8,128)S(1)} %get-tuple-element.37), channel_id=1, source_target_pairs={{0,8},{8,0},{16,24},{24,16},{1,9},{9,1},{17,25},{25,17},{2,10},{10... | collective-permute-start | bytes 221192 | tf_op jit(solution)/shard_map/ppermute | solution.py:623
  30.6 11.7 %collective-permute-start.3 = (f32[9,16,128]{2,1,0:T(8,128)S(1)}, f32[9,16,128]{2,1,0:T(8,128)S(1)}, u32[]{:S(2)}, u32[]{:S(2)}) collective-permute-start(f32[9,16,128]{2,1,0:T(8,128)S(1)} %get-tuple-element.38), channel_id=1, source_target_pairs={{0,24},{8,16},{16,8},{24,0},{1,25},{9,17},{17,9},{25,1},{2,26},{10... | collective-permute-start | bytes 221192 | tf_op jit(solution)/shard_map/ppermute | solution.py:622
  31.9 15.1 %collective-permute-start.12 = (f32[80,128]{1,0:T(8,128)S(1)}, f32[80,128]{1,0:T(8,128)S(1)}, u32[]{:S(2)}, u32[]{:S(2)}) collective-permute-start(f32[80,128]{1,0:T(8,128)S(1)} %get-tuple-element.63), channel_id=1, source_target_pairs={{0,1},{1,0},{2,3},{3,2},{4,5},{5,4},{6,7},{7,6},{8,9},{9,8},{10,11... | collective-permute-start | bytes 122888 | tf_op jit(solution)/shard_map/ppermute | solution.py:623
  36.0 11.0 %collective-permute-start.13 = (f32[80,128]{1,0:T(8,128)S(1)}, f32[80,128]{1,0:T(8,128)S(1)}, u32[]{:S(2)}, u32[]{:S(2)}) collective-permute-start(f32[80,128]{1,0:T(8,128)S(1)} %get-tuple-element.64), channel_id=1, source_target_pairs={{0,7},{1,2},{2,1},{3,4},{4,3},{5,6},{6,5},{7,0},{8,15},{9,10},{10,... | collective-permute-start | bytes 122888 | tf_op jit(solution)/shard_map/ppermute | solution.py:622

commit v2 on v1

--- a/solution.py
+++ b/solution.py
@@ -152,25 +152,22 @@
     w[:, half:] = full
 
 
-def first_body(pop, spec, react_in, kc_in, rk_in, mix_in, sv, w, ma, mb, ya, yb, c03, s03,
-               fixed, u, post, rx, kc, rk, mix, rt, odd, keep, rv, psem, ssem, tsem, pv):
+def first_body(pop, spec, react_in, kc_in, rk_in, mix_in, pv, sv, w, ma, mb, c03, s03, fixed,
+               rx, kc, rk, mix, rt, rv, psem, ssem, tsem):
     planes, rows, lanes = pop.shape[1:]
     species = spec.shape[1]
     ends = (0, planes - 1)
-    inner = range(1, planes - 1)
     small = [
         pltpu.make_async_copy(src, dst, tsem.at[n])
         for n, (src, dst) in enumerate(
             ((react_in, rv), (react_in, rx), (kc_in, kc), (rk_in, rk), (mix_in, mix))
         )
     ]
-    kinds = [pltpu.make_async_copy(spec.at[:, :, x], sv.at[:, :, x], ssem.at[x])
-             for x in range(planes)]
-    flows = [pltpu.make_async_copy(pop.at[:, x], pv.at[:, x], psem.at[x]) for x in range(planes)]
-    for copy in small + [kinds[x] for x in ends] + flows + [kinds[x] for x in inner]:
+    order = ends + tuple(range(1, planes - 1))
+    kinds = [pltpu.make_async_copy(spec.at[:, :, x], sv.at[:, :, x], ssem.at[x]) for x in order]
+    flows = [pltpu.make_async_copy(pop.at[:, x], pv.at[:, x], psem.at[x]) for x in order]
+    for copy in small + kinds[:2] + flows + kinds[2:]:
         copy.start()
-    for k in range(species):
-        c03[k, 2 * rows :, :] = jnp.zeros((c03.shape[1] - 2 * rows, lanes), F32)
     for copy in small:
         copy.wait()
     stoichiometry(rv, w)
@@ -181,7 +178,7 @@
         for n, i in enumerate((0, 1, 3, 4)):
             fixed[3 + 4 * side + n] = inlet_weight(i, side) * fixed[1 + side]
     for n, x in enumerate(ends):
-        kinds[x].wait()
+        kinds[n].wait()
 
         def conc(k, carry, n=n, x=x):
             total = sv[0, k, x]
@@ -190,16 +187,26 @@
             c03[k, n * rows : (n + 1) * rows, :] = total
             return carry
 
-        lax.fori_loop(0, species, conc, 0, unroll=5)
-    react(rx, kc, c03, s03, w, rt, start=0, stop=2 * rows)
-    for copy in flows:
+        lax.fori_loop(0, species, conc, 0, unroll=CONC)
+    react(rx, kc, c03, s03, w, rt)
+    speeds = []
+    for n, x in enumerate(ends):
+        flows[n].wait()
+        speeds.append(moments([pv[q, x] for q in range(27)])[1][0])
+    send_faces(sv, rk, c03, s03, speeds, ma, mb)
+    for copy in flows[2:] + kinds[2:]:
         copy.wait()
+
+
+def second_body(pv, sv, c03, s03, rx, kc, w, fixed, u, post, ya, yb, edge_c, edge_s, odd, keep):
+    species, planes, rows, lanes = sv.shape[1:]
+    inner = range(1, planes - 1)
+    for k in range(species):
+        edge_c[k] = jnp.zeros(edge_c.shape[1:], F32)
     collide_flow(pv, u, post)
-    for x in inner:
-        kinds[x].wait()
     flat = sv.reshape(7 * species * planes * rows, lanes)
-    height = c03.shape[1]
-    cflat = c03.reshape(species * height, lanes)
+    height = edge_c.shape[1]
+    cflat = edge_c.reshape(species * height, lanes)
     for x in inner:
         for side, row in ((0, 0), (1, rows - 1)):
             for k, size in bands(species):
@@ -210,12 +217,11 @@
                 total = values[0]
                 for i in range(1, 7):
                     total = total + values[i]
-                spot = 2 * rows + 2 * (x - 1) + side
-                cflat[pl.ds(k * height + spot, size, height), :] = total
+                spot = k * height + 2 * (x - 1) + side
+                cflat[pl.ds(spot, size, height), :] = total
                 keep[side, x * species + k : x * species + k + size, :] = values[3 if side else 4]
-    react(rx, kc, c03, s03, w, rt, odd, start=2 * rows)
-    send_faces(sv, rk, c03, s03, [u[0, x] for x in ends], ma, mb)
-    send_rows(sv, keep, c03, s03, fixed, u, ya, yb)
+    react(rx, kc, edge_c, edge_s, w, None, odd)
+    send_rows(sv, keep, c03, s03, edge_c, edge_s, fixed, u, ya, yb)
     first, last, even = edge_flags()
     for n in range(9):
         for x in range(planes):
@@ -231,25 +237,29 @@
     return rank == 0, rank == size - 1, is_even("gy")
 
 
-def send_rows(state, keep, c03, s03, fixed, u, ya, yb):
+def send_rows(state, keep, c03, s03, edge_c, edge_s, fixed, u, ya, yb):
     species, planes, rows, lanes = state.shape[1:]
-    height = c03.shape[1]
     fresh = state.reshape(7 * species * planes * rows, lanes)
-    cflat = c03.reshape(species * height, lanes)
-    sflat = s03.reshape(species * height, lanes)
     first, last, even = edge_flags()
     for x in range(planes):
+        if x in (0, planes - 1):
+            cref, sref, base = c03, s03, (x > 0) * rows
+        else:
+            cref, sref, base = edge_c, edge_s, 2 * (x - 1)
+        height = cref.shape[1]
+        cflat = cref.reshape(species * height, lanes)
+        sflat = sref.reshape(species * height, lanes)
         for k, size in bands(species):
             halo = slice(x * species + k, x * species + k + size)
             sent = []
             for side, row, off in ((0, 0, first), (1, rows - 1, last)):
                 i, sign = (3, 1.0) if side else (4, -1.0)
                 if x in (0, planes - 1):
-                    spot = (x > 0) * rows + row
+                    spot = base + row
                     at = ((i * species + k) * planes + x) * rows + row
                     value = fresh[pl.ds(at, size, planes * rows), :]
                 else:
-                    spot = 2 * rows + 2 * (x - 1) + side
+                    spot = base + side
                     value = keep[side, halo, :]
                 c = cflat[pl.ds(k * height + spot, size, height), :]
                 s = sflat[pl.ds(k * height + spot, size, height), :]
@@ -359,25 +369,22 @@
     return {0: 0.25, 3: 0.125 * (1.0 + tilt), 4: 0.125 * (1.0 - tilt)}.get(i, 0.125)
 
 
-def edge_body(g, hxa, hxb, hya, hyb, nt, u, rx, kc, rk, w, fixed, new, ma, mb, ya, yb, c03, s03,
-              rt, odd, keep):
-    hx, hy = Halo(hxa, hxb, "gx"), Halo(hya, hyb, "gy")
+def ready_body(g, hya, hyb, nt, rx, kc, w, fixed, new, c03, keep, edge_c, edge_s, odd):
+    hy = Halo(hya, hyb, "gy")
     species, planes, rows, lanes = g.shape[1:]
-    height = c03.shape[1]
-    ends = (0, planes - 1)
     flat = g.reshape(7 * species * planes * rows, lanes)
-    cflat = c03.reshape(species * height, lanes)
-    jump = planes * rows
-    zeros = height - 2 * rows
+    height = edge_c.shape[1]
+    cflat = edge_c.reshape(species * height, lanes)
     for k in range(species):
-        c03[k, 2 * rows :, :] = jnp.zeros((zeros, lanes), F32)
+        edge_c[k] = jnp.zeros((height, lanes), F32)
     for x in range(1, planes - 1):
         for side, row in ((0, 0), (1, rows - 1)):
             kind = nt[x, row : row + 1, :]
             for k, size in bands(species):
 
                 def load(i, plane, r, k=k, size=size):
-                    return flat[pl.ds(((i * species + k) * planes + plane) * rows + r, size, jump), :]
+                    at = ((i * species + k) * planes + plane) * rows + r
+                    return flat[pl.ds(at, size, planes * rows), :]
 
                 halo = slice(x * species + k, x * species + k + size)
                 moved = {
@@ -399,27 +406,48 @@
                 i = 3 if side else 4
                 kept = jnp.where(wide == 1, moved[7 - i], moved[i])
                 kept = jnp.where(inlet, inlet_weight(i, side) * value, kept)
-                spot = 2 * rows + 2 * (x - 1) + side
-                cflat[pl.ds(k * height + spot, size, height), :] = total
+                spot = k * height + 2 * (x - 1) + side
+                cflat[pl.ds(spot, size, height), :] = total
                 keep[side, halo, :] = kept
+    for n, x in enumerate((0, planes - 1)):
+        kind = masks(nt, x)
+
+        def step(k, carry, n=n, x=x, kind=kind):
+            moved = gather(k, x, g, None, hy, (0, 3, 5))
+            total = g[2, k, 1] if n == 0 else g[1, k, planes - 2]
+            for m in moved.values():
+                total = total + m
+            for i, value in walled(moved, kind, k, fixed).items():
+                new[i, k, x] = value
+            c03[k, n * rows : (n + 1) * rows, :] = total
+            return carry
+
+        lax.fori_loop(0, species, step, 0, unroll=CONC)
+    react(rx, kc, edge_c, edge_s, w, None, odd)
+
+
+def edge_body(g, hxa, hxb, nt, u, rx, kc, rk, w, fixed, keep, edge_c, edge_s, new_in, part, new,
+              c03, ma, mb, ya, yb, s03, rt):
+    del new_in, part
+    hx = Halo(hxa, hxb, "gx")
+    species, planes, rows, _ = g.shape[1:]
+    ends = (0, planes - 1)
     for n, x in enumerate(ends):
         kind = masks(nt, x)
 
         def step(k, carry, n=n, x=x, kind=kind):
-            moved = gather(k, x, g, hx, hy, (0, 1, 3, 5))
-            values = walled(moved, kind, k, fixed)
-            total = moved[0]
-            for i in range(1, 7):
-                total = total + moved[i]
-            for i in range(7):
-                new[i, k, x] = values[i]
-            c03[k, n * rows : (n + 1) * rows, :] = settle(total, kind, k, fixed, (1, 2))
+            moved = gather(k, x, g, hx, None, (1,))
+            part = slice(n * rows, (n + 1) * rows)
+            total = c03[k, part, :] + moved[1 + n]
+            for i, value in walled(moved, kind, k, fixed).items():
+                new[i, k, x] = value
+            c03[k, part, :] = settle(total, kind, k, fixed, (1, 2))
             return carry
 
         lax.fori_loop(0, species, step, 0, unroll=CONC)
-    react(rx, kc, c03, s03, w, rt, odd)
+    react(rx, kc, c03, s03, w, rt)
     send_faces(new, rk, c03, s03, [u[0, x] for x in ends], ma, mb)
-    send_rows(new, keep, c03, s03, fixed, u, ya, yb)
+    send_rows(new, keep, c03, s03, edge_c, edge_s, fixed, u, ya, yb)
 
 
 def rest_body(moving, final, *refs):
@@ -610,9 +638,9 @@
     state = arr(7, count, planes, rows, lanes)
     inner = planes - 2
     edges = -(-2 * inner // 8) * 8
-    wide = (2 * rows + edges) // 8
-    react_out = arr(count, 2 * rows + edges, lanes)
-    rates = VMEM((2 * total * 8, wide // 2 * 2 * lanes), BF16)
+    edge_out = arr(count, edges, lanes)
+    react_out = arr(count, 2 * rows, lanes)
+    rates = VMEM((2 * total * 8, 2 * rows // 8 * lanes), BF16)
     odd = VMEM((total * 8, 2 * lanes), BF16)
     rates_in = VMEM((2 * total * 8, inner * rows // 8 * lanes), BF16)
     inside = VMEM((count, inner * rows, lanes), F32)
@@ -628,20 +656,27 @@
     ints = pltpu.SMEM((3, total), jnp.int32)
     flows = arr(27, planes, rows, lanes)
     ymsg = arr((count + 9) * planes, lanes)
-    keep = VMEM((2, count * planes, lanes), F32)
-    sv, w, ma, mb, ya, yb, c03, s03, fixed, u, post, *tables = call(
+    keep = arr(2, count * planes, lanes)
+    pv, sv, w, ma, mb, c03, s03, fixed, *tables = call(
         first_body,
         [hbm(v) for v in (populations, species, reactions.T, rate_const, species_rate, inlet_mix)],
         [ANY] * 6,
-        (flows, state, VMEM((count * 8, 2 * total * 8), BF16), xmsg, xmsg, ymsg, ymsg, react_out,
-         react_out, arr(11, count, lanes), arr(3, planes, rows, lanes), flows, ints,
-         pltpu.SMEM((total,), F32), pltpu.SMEM((count,), F32))[1:],
-        [VM] * 11 + [SM] * 3,
-        [pltpu.SMEM((2, count), F32), rates, odd, keep, VMEM((3, total), jnp.int32)] + sems
-        + [pltpu.SemaphoreType.DMA((5,)), flows],
+        (flows, state, VMEM((count * 8, 2 * total * 8), BF16), xmsg, xmsg, react_out, react_out,
+         arr(11, count, lanes), ints, pltpu.SMEM((total,), F32), pltpu.SMEM((count,), F32)),
+        [VM] * 8 + [SM] * 3,
+        [pltpu.SMEM((2, count), F32), rates, VMEM((3, total), jnp.int32)] + sems
+        + [pltpu.SemaphoreType.DMA((5,))],
     )
     tables = [pltpu.with_memory_space_constraint(v, pltpu.SMEM) for v in tables]
     hx = swap(ma, mb, "gx")
+    u, post, ya, yb = call(
+        second_body,
+        [inv(v) for v in (pv, sv, c03, s03)] + tables[:2] + [inv(w), inv(fixed)],
+        [VM] * 4 + [SM] * 2 + [VM] * 2,
+        (arr(3, planes, rows, lanes), flows, ymsg, ymsg),
+        [VM] * 4,
+        [edge_out, edge_out, odd, keep],
+    )
     hy = swap(ya, yb, "gy")
     ymsg = arr(count * planes, lanes)
     flow_hy = hy
@@ -651,13 +686,23 @@
         moving = s > 0
         if moving:
             halo = hy
-            new, ma, mb, ya, yb, c03, s03 = call(
+            new, c03, kept, edge_c, edge_s = call(
+                ready_body,
+                [inv(v) for v in (g, *hy, node_type)] + tables[:2] + [inv(w), inv(fixed)],
+                [VM] * 4 + [SM] * 2 + [VM] * 2,
+                (state, react_out, keep, edge_out, edge_out),
+                [VM] * 5,
+                [odd],
+            )
+            new, c03, ma, mb, ya, yb, s03 = call(
                 edge_body,
-                [inv(v) for v in (g, *hx, *hy, node_type, u)] + tables + [inv(w), inv(fixed)],
-                [VM] * 7 + smem + [VM] * 2,
-                (state, xmsg, xmsg, ymsg, ymsg, react_out, react_out),
+                [inv(v) for v in (g, *hx, node_type, u)] + tables
+                + [inv(v) for v in (w, fixed, kept, edge_c, edge_s, new, c03)],
+                [VM] * 5 + smem + [VM] * 7,
+                (state, react_out, xmsg, xmsg, ymsg, ymsg, react_out),
                 [VM] * 7,
-                [rates, odd, keep],
+                [rates],
+                alias={13: 0, 14: 1},
             )
             hx = swap(ma, mb, "gx")
             hy = swap(ya, yb, "gy")

time: 48.8 us -> 47.1 us (0.965)
  waiting for transfers between devices: 4.41 us -> 2.97 us
    ppermute x7, waiting for transfers between devices: 4.19 us -> 2.54 us  [swap(): far = lax.ppermute(far, axis, pairs(size, False))]
    pallas_call x9 -> x12, Pallas kernels: 16.6 us -> 16.4 us  [call(): pl.pallas_call(body, out_shape=outs, in_specs=specs, out_specs=out_specs,...]
  transfers between devices with their start and end apart: 14 -> 14, of which waited for: 4 -> 4; matrix products, arithmetic and copies ran while one was open for 0% -> 0% of each run, Pallas kernels for 17% -> 21%
where the time goes in v2:
time: 47.1 us; the launch traced here: 46.9 us
  starting transfers between devices  26.8 us (57%)
  Pallas kernels  16.4 us (35%)
  waiting for transfers between devices  2.97 us (6%)
  between operations  0.79 us (2%)
    ppermute x7, starting transfers between devices, swap(): far = lax.ppermute(far, axis, pairs(size, False))  16.9 us
    pallas_call x12, Pallas kernels, call(): pl.pallas_call(body, out_shape=outs, in_specs=specs, out_specs=out_specs,...  16.4 us
    ppermute x7, starting transfers between devices, swap(): near = lax.ppermute(near, axis, pairs(size, True))  9.9 us
    ppermute x7, waiting for transfers between devices, swap(): far = lax.ppermute(far, axis, pairs(size, False))  2.54 us
  transfers between devices with their start and end apart: 14, of which 4 were waited for; matrix products, arithmetic and copies ran while one was open for 0% of the time, Pallas kernels for 21%

profile of v2, /device:TPU:1, one launch (start us, length us, event | category | flops | bytes accessed | tf_op | source)
XLA Modules:
  0.0 46.9 jit_solution(17254315541422362639)
XLA Ops:
  0.6 2.7 %shard_map.86 = (f32[27,4,16,128]{3,2,1,0:T(8,128)S(1)}, f32[7,20,4,16,128]{4,3,2,1,0:T(8,128)S(1)}, bf16[160,1344]{1,0:T(8,128)(2,1)S(1)}, f32[20,16,128]{2,1,0...) custom-call(f32[27,4,16,128]{3,2,1,0:T(8,128)} %pop.1, ...), custom_call_target="tpu_custom_call" | custom-call | flops 2000000 | bytes 2000000 | tf_op jit(solution)/shard_map/pallas_call | solution.py:64
  3.4 2.2 %collective-permute-start.4 = (f32[20,16,128]{2,1,0:T(8,128)S(1)}, f32[20,16,128]{2,1,0:T(8,128)S(1)}, u32[]{:S(2)}, u32[]{:S(2)}) collective-permute-start(f32[20,16,128]{2,1,0:T(8,128)S(1)} %get-tuple-element.60), channel_id=1, source_target_pairs={{0,8},{8,0},{16,24},{24,16},{1,9},{9,1},{17,25},{25,17},{2,10},{10... | collective-permute-start | bytes 491528 | tf_op jit(solution)/shard_map/ppermute | solution.py:651
  5.6 2.2 %collective-permute-start.5 = (f32[20,16,128]{2,1,0:T(8,128)S(1)}, f32[20,16,128]{2,1,0:T(8,128)S(1)}, u32[]{:S(2)}, u32[]{:S(2)}) collective-permute-start(f32[20,16,128]{2,1,0:T(8,128)S(1)} %get-tuple-element.61), channel_id=1, source_target_pairs={{0,24},{8,16},{16,8},{24,0},{1,25},{9,17},{17,9},{25,1},{2,26},{10... | collective-permute-start | bytes 491528 | tf_op jit(solution)/shard_map/ppermute | solution.py:650
  7.7 0.9 %shard_map.87 = (f32[3,4,16,128]{3,2,1,0:T(8,128)S(1)}, f32[27,4,16,128]{3,2,1,0:T(8,128)S(1)}, f32[116,128]{1,0:T(8,128)S(1)}, f32[116,128]{1,0:T(8,128)S(1)}) custom-call(f32[27,4,16,128]{3,2,1,0:T(8,128)S(1)} %get-tuple-element.45.pv, f32[7,20,4,16,128]{4,3,2,1,0:T(8,128)S(1)} %get-tuple-element.46.sv.refs_0_, ...), custom_call_target="tpu_custom_call" | custom-call | flops 2000000 | bytes 2000000 | tf_op jit(solution)/shard_map/pallas_call | solution.py:64
  8.7 1.3 %collective-permute-start = (f32[116,128]{1,0:T(8,128)S(1)}, f32[116,128]{1,0:T(8,128)S(1)}, u32[]{:S(2)}, u32[]{:S(2)}) collective-permute-start(f32[116,128]{1,0:T(8,128)S(1)} %get-tuple-element.54), channel_id=1, source_target_pairs={{0,1},{1,0},{2,3},{3,2},{4,5},{5,4},{6,7},{7,6},{8,9},{9,8},{10,11... | collective-permute-start | bytes 178184 | tf_op jit(solution)/shard_map/ppermute | solution.py:651
  10.0 1.2 %collective-permute-start.1 = (f32[116,128]{1,0:T(8,128)S(1)}, f32[116,128]{1,0:T(8,128)S(1)}, u32[]{:S(2)}, u32[]{:S(2)}) collective-permute-start(f32[116,128]{1,0:T(8,128)S(1)} %get-tuple-element.55), channel_id=1, source_target_pairs={{0,7},{1,2},{2,1},{3,4},{4,3},{5,6},{6,5},{7,0},{8,15},{9,10},{10,... | collective-permute-start | bytes 178184 | tf_op jit(solution)/shard_map/ppermute | solution.py:650
  11.2 1.6 %shard_map.90.g.refs_0_ = f32[7,20,4,16,128]{4,3,2,1,0:T(8,128)S(1)} custom-call(f32[7,20,4,16,128]{4,3,2,1,0:T(8,128)S(1)} %get-tuple-element.46.sv.refs_0_, f32[20,32,128]{2,1,0:T(8,128)S(1)} %get-tuple-element.47.c03.refs_1_, f32[20,32,128]{2,1,0:T(8,128)S(1)} %get-tuple-element.48.s03.refs_2_, ...), custom_call_target="tpu_custom_call", output_to_operand_aliasing={{}: (0, {})} | custom-call | flops 2000000 | bytes 2000000 | tf_op jit(solution)/shard_map/pallas_call | solution.py:64
  12.8 0.0 collective-permute-done.hya.refs_9_
  12.8 1.5 %collective-permute-done.1.hyb.refs_10_ = f32[116,128]{1,0:T(8,128)S(1)} collective-permute-done((f32[116,128]{1,0:T(8,128)S(1)}, f32[116,128]{1,0:T(8,128)S(1)}, u32[]{:S(2)}, u32[]{:S(2)}) %collective-permute-start.1) | collective-permute-done | bytes 59424 | tf_op jit(solution)/shard_map/ppermute | solution.py:650
  14.3 0.6 %shard_map.91 = (f32[7,20,4,16,128]{4,3,2,1,0:T(8,128)S(1)}, f32[20,32,128]{2,1,0:T(8,128)S(1)}, f32[2,80,128]{2,1,0:T(8,128)S(1)}, f32[20,8,128]{2,1,0:T(8,128)S(1)}, f32[20,8,128]{2,1,0:T(8,128)S(1)}) custom-call(f32[7,20,4,16,128]{4,3,2,1,0:T(8,128)S(1)} %shard_map.90.g.refs_0_, f32[116,128]{1,0:T(8,128)S(1)} %collective-permute-done.hya.refs_9_, ...), custom_call_target="tpu_custom_call" | custom-call | flops 2000000 | bytes 2000000 | tf_op jit(solution)/shard_map/pallas_call | solution.py:64
  14.8 0.0 collective-permute-done.4.hxa
  14.8 0.1 collective-permute-done.5.hxb
  14.9 1.0 %shard_map.92 = (f32[7,20,4,16,128]{4,3,2,1,0:T(8,128)S(1)}, f32[20,32,128]{2,1,0:T(8,128)S(1)}, f32[20,16,128]{2,1,0:T(8,128)S(1)}, f32[20,16,128]{2,1,0:T(8,12...) custom-call(f32[7,20,4,16,128]{4,3,2,1,0:T(8,128)S(1)} %shard_map.90, ...), custom_call_target="tpu_custom_call", output_to_operand_aliasing={{0}: (13, {}), {1}: (14, {})} | custom-call | flops 2000000 | bytes 2000000 | tf_op jit(solution)/shard_map/pallas_call | solution.py:64
  15.9 0.4 collective-permute-start.6
  16.3 2.3 %collective-permute-start.7 = (f32[20,16,128]{2,1,0:T(8,128)S(1)}, f32[20,16,128]{2,1,0:T(8,128)S(1)}, u32[]{:S(2)}, u32[]{:S(2)}) collective-permute-start(f32[20,16,128]{2,1,0:T(8,128)S(1)} %get-tuple-element.71), channel_id=1, source_target_pairs={{0,24},{8,16},{16,8},{24,0},{1,25},{9,17},{17,9},{25,1},{2,26},{10... | collective-permute-start | bytes 491528 | tf_op jit(solution)/shard_map/ppermute | solution.py:650
  18.6 2.1 %collective-permute-start.8 = (f32[80,128]{1,0:T(8,128)S(1)}, f32[80,128]{1,0:T(8,128)S(1)}, u32[]{:S(2)}, u32[]{:S(2)}) collective-permute-start(f32[80,128]{1,0:T(8,128)S(1)} %get-tuple-element.72), channel_id=1, source_target_pairs={{0,1},{1,0},{2,3},{3,2},{4,5},{5,4},{6,7},{7,6},{8,9},{9,8},{10,11... | collective-permute-start | bytes 122888 | tf_op jit(solution)/shard_map/ppermute | solution.py:651
  20.8 1.1 %collective-permute-start.9 = (f32[80,128]{1,0:T(8,128)S(1)}, f32[80,128]{1,0:T(8,128)S(1)}, u32[]{:S(2)}, u32[]{:S(2)}) collective-permute-start(f32[80,128]{1,0:T(8,128)S(1)} %get-tuple-element.73), channel_id=1, source_target_pairs={{0,7},{1,2},{2,1},{3,4},{4,3},{5,6},{6,5},{7,0},{8,15},{9,10},{10,... | collective-permute-start | bytes 122888 | tf_op jit(solution)/shard_map/ppermute | solution.py:650
  21.9 1.8 %shard_map.93.g.refs_0_ = f32[7,20,4,16,128]{4,3,2,1,0:T(8,128)S(1)} custom-call(f32[7,20,4,16,128]{4,3,2,1,0:T(8,128)S(1)} %shard_map.90.g.refs_0_, f32[7,20,4,16,128]{4,3,2,1,0:T(8,128)S(1)} %get-tuple-element.67.refs_1_, f32[20,32,128]{2,1,0:T(8,128)S(1)} %get-tuple-element.68.refs_2_, ...), custom_call_target="tpu_custom_call", output_to_operand_aliasing={{}: (1, {})} | custom-call | flops 2000000 | bytes 2000000 | tf_op jit(solution)/shard_map/pallas_call | solution.py:64
  23.7 1.0 %collective-permute-done.9.hyb.refs_10_ = f32[80,128]{1,0:T(8,128)S(1)} collective-permute-done((f32[80,128]{1,0:T(8,128)S(1)}, f32[80,128]{1,0:T(8,128)S(1)}, u32[]{:S(2)}, u32[]{:S(2)}) %collective-permute-start.9) | collective-permute-done | bytes 40992 | tf_op jit(solution)/shard_map/ppermute | solution.py:650
  24.7 0.6 %shard_map.94 = (f32[7,20,4,16,128]{4,3,2,1,0:T(8,128)S(1)}, f32[20,32,128]{2,1,0:T(8,128)S(1)}, f32[2,80,128]{2,1,0:T(8,128)S(1)}, f32[20,8,128]{2,1,0:T(8,128)S(1)}, f32[20,8,128]{2,1,0:T(8,128)S(1)}) custom-call(f32[7,20,4,16,128]{4,3,2,1,0:T(8,128)S(1)} %shard_map.93.g.refs_0_, f32[80,128]{1,0:T(8,128)S(1)} %collective-permute-done.8.hya.refs_9_, ...), custom_call_target="tpu_custom_call" | custom-call | flops 2000000 | bytes 2000000 | tf_op jit(solution)/shard_map/pallas_call | solution.py:64
  25.3 0.0 collective-permute-done.7.hxb
  25.3 1.0 %shard_map.95 = (f32[7,20,4,16,128]{4,3,2,1,0:T(8,128)S(1)}, f32[20,32,128]{2,1,0:T(8,128)S(1)}, f32[20,16,128]{2,1,0:T(8,128)S(1)}, f32[20,16,128]{2,1,0:T(8,12...) custom-call(f32[7,20,4,16,128]{4,3,2,1,0:T(8,128)S(1)} %shard_map.93, ...), custom_call_target="tpu_custom_call", output_to_operand_aliasing={{0}: (13, {}), {1}: (14, {})} | custom-call | flops 2000000 | bytes 2000000 | tf_op jit(solution)/shard_map/pallas_call | solution.py:64
  26.3 0.1 collective-permute-start.10
  26.3 1.4 %collective-permute-start.11 = (f32[20,16,128]{2,1,0:T(8,128)S(1)}, f32[20,16,128]{2,1,0:T(8,128)S(1)}, u32[]{:S(2)}, u32[]{:S(2)}) collective-permute-start(f32[20,16,128]{2,1,0:T(8,128)S(1)} %get-tuple-element.84), channel_id=1, source_target_pairs={{0,24},{8,16},{16,8},{24,0},{1,25},{9,17},{17,9},{25,1},{2,26},{10... | collective-permute-start | bytes 491528 | tf_op jit(solution)/shard_map/ppermute | solution.py:650
  27.8 0.6 %collective-permute-start.2 = (f32[9,16,128]{2,1,0:T(8,128)S(1)}, f32[9,16,128]{2,1,0:T(8,128)S(1)}, u32[]{:S(2)}, u32[]{:S(2)}) collective-permute-start(f32[9,16,128]{2,1,0:T(8,128)S(1)} %get-tuple-element.56), channel_id=1, source_target_pairs={{0,8},{8,0},{16,24},{24,16},{1,9},{9,1},{17,25},{25,17},{2,10},{10... | collective-permute-start | bytes 221192 | tf_op jit(solution)/shard_map/ppermute | solution.py:651
  28.4 1.9 %collective-permute-start.3 = (f32[9,16,128]{2,1,0:T(8,128)S(1)}, f32[9,16,128]{2,1,0:T(8,128)S(1)}, u32[]{:S(2)}, u32[]{:S(2)}) collective-permute-start(f32[9,16,128]{2,1,0:T(8,128)S(1)} %get-tuple-element.57), channel_id=1, source_target_pairs={{0,24},{8,16},{16,8},{24,0},{1,25},{9,17},{17,9},{25,1},{2,26},{10... | collective-permute-start | bytes 221192 | tf_op jit(solution)/shard_map/ppermute | solution.py:650
  30.2 3.2 %collective-permute-start.12 = (f32[80,128]{1,0:T(8,128)S(1)}, f32[80,128]{1,0:T(8,128)S(1)}, u32[]{:S(2)}, u32[]{:S(2)}) collective-permute-start(f32[80,128]{1,0:T(8,128)S(1)} %get-tuple-element.85), channel_id=1, source_target_pairs={{0,1},{1,0},{2,3},{3,2},{4,5},{5,4},{6,7},{7,6},{8,9},{9,8},{10,11... | collective-permute-start | bytes 122888 | tf_op jit(solution)/shard_map/ppermute | solution.py:651
  33.5 0.4 collective-permute-done.2.fxa
  33.9 6.7 %collective-permute-start.13 = (f32[80,128]{1,0:T(8,128)S(1)}, f32[80,128]{1,0:T(8,128)S(1)}, u32[]{:S(2)}, u32[]{:S(2)}) collective-permute-start(f32[80,128]{1,0:T(8,128)S(1)} %get-tuple-element.86), channel_id=1, source_target_pairs={{0,7},{1,2},{2,1},{3,4},{4,3},{5,6},{6,5},{7,0},{8,15},{9,10},{10,... | collective-permute-start | bytes 122888 | tf_op jit(solution)/shard_map/ppermute | solution.py:650
  40.6 1.1 %shard_map.89 = f32[27,4,16,128]{3,2,1,0:T(8,128)} custom-call(f32[27,4,16,128]{3,2,1,0:T(8,128)S(1)} %get-tuple-element.53.post, f32[9,16,128]{2,1,0:T(8,128)S(1)} %collective-permute-done.2.fxa, f32[9,16,128]{2,1,0:T(8,128)S(1)} %collective-permute-done.3.fxb, f32[116,128]{1,0:T(8,128)S(1)} %collective-permute-done.hya.refs_9_, ...), custom_call_target="tpu_custom_call" | custom-call | flops 2000000 | bytes 2000000 | tf_op jit(solution)/shard_map/pallas_call | solution.py:64
  41.7 3.5 %shard_map.96 = (f32[7,20,4,16,128]{4,3,2,1,0:T(8,128)S(1)}, f32[7,20,4,16,128]{4,3,2,1,0:T(8,128)}) custom-call(f32[7,20,4,16,128]{4,3,2,1,0:T(8,128)S(1)} %shard_map.93.g.refs_0_, f32[7,20,4,16,128]{4,3,2,1,0:T(8,128)S(1)} %get-tuple-element.79.refs_1_, f32[20,32,128]{2,1,0:T(8,128)S(1)} %get-tuple-element.80.refs_2_, ...), custom_call_target="tpu_custom_call", output_to_operand_aliasing={{0}: (1, {})} | custom-call | flops 2000000 | bytes 2000000 | tf_op jit(solution)/shard_map/pallas_call | solution.py:64
  45.3 1.6 %shard_map.97 = f32[7,20,4,16,128]{4,3,2,1,0:T(8,128)} custom-call(f32[7,20,4,16,128]{4,3,2,1,0:T(8,128)S(1)} %get-tuple-element.82.g, f32[20,16,128]{2,1,0:T(8,128)S(1)} %collective-permute-done.10.hxa, f32[20,16,128]{2,1,0:T(8,128)S(1)} %collective-permute-done.11.hxb, f32[80,128]{1,0:T(8,128)S(1)} %collective-permute-done.12.hya, ...), custom_call_target="tpu_custom_call", output_to_operand_aliasing={{}: (7, {})} | custom-call | flops 2000000 | bytes 2000000 | tf_op jit(solution)/shard_map/pallas_call | solution.py:64
  (10 shorter events, 0.0 us)
Async XLA Ops:
  3.4 11.5 %collective-permute-start.4 = (f32[20,16,128]{2,1,0:T(8,128)S(1)}, f32[20,16,128]{2,1,0:T(8,128)S(1)}, u32[]{:S(2)}, u32[]{:S(2)}) collective-permute-start(f32[20,16,128]{2,1,0:T(8,128)S(1)} %get-tuple-element.60), channel_id=1, source_target_pairs={{0,8},{8,0},{16,24},{24,16},{1,9},{9,1},{17,25},{25,17},{2,10},{10... | collective-permute-start | bytes 491528 | tf_op jit(solution)/shard_map/ppermute | solution.py:651
  5.6 9.4 %collective-permute-start.5 = (f32[20,16,128]{2,1,0:T(8,128)S(1)}, f32[20,16,128]{2,1,0:T(8,128)S(1)}, u32[]{:S(2)}, u32[]{:S(2)}) collective-permute-start(f32[20,16,128]{2,1,0:T(8,128)S(1)} %get-tuple-element.61), channel_id=1, source_target_pairs={{0,24},{8,16},{16,8},{24,0},{1,25},{9,17},{17,9},{25,1},{2,26},{10... | collective-permute-start | bytes 491528 | tf_op jit(solution)/shard_map/ppermute | solution.py:650
  8.7 4.1 %collective-permute-start = (f32[116,128]{1,0:T(8,128)S(1)}, f32[116,128]{1,0:T(8,128)S(1)}, u32[]{:S(2)}, u32[]{:S(2)}) collective-permute-start(f32[116,128]{1,0:T(8,128)S(1)} %get-tuple-element.54), channel_id=1, source_target_pairs={{0,1},{1,0},{2,3},{3,2},{4,5},{5,4},{6,7},{7,6},{8,9},{9,8},{10,11... | collective-permute-start | bytes 178184 | tf_op jit(solution)/shard_map/ppermute | solution.py:651
  10.0 4.3 %collective-permute-start.1 = (f32[116,128]{1,0:T(8,128)S(1)}, f32[116,128]{1,0:T(8,128)S(1)}, u32[]{:S(2)}, u32[]{:S(2)}) collective-permute-start(f32[116,128]{1,0:T(8,128)S(1)} %get-tuple-element.55), channel_id=1, source_target_pairs={{0,7},{1,2},{2,1},{3,4},{4,3},{5,6},{6,5},{7,0},{8,15},{9,10},{10,... | collective-permute-start | bytes 178184 | tf_op jit(solution)/shard_map/ppermute | solution.py:650
  11.2 3.1 %copy-start = (s32[4,16,128]{2,1,0:T(8,128)S(1)}, s32[4,16,128]{2,1,0:T(8,128)}, u32[]{:S(2)}) copy-start(s32[4,16,128]{2,1,0:T(8,128)} %nt.11) | copy-start | bytes 98308
  15.9 9.3 %collective-permute-start.6 = (f32[20,16,128]{2,1,0:T(8,128)S(1)}, f32[20,16,128]{2,1,0:T(8,128)S(1)}, u32[]{:S(2)}, u32[]{:S(2)}) collective-permute-start(f32[20,16,128]{2,1,0:T(8,128)S(1)} %get-tuple-element.70), channel_id=1, source_target_pairs={{0,8},{8,0},{16,24},{24,16},{1,9},{9,1},{17,25},{25,17},{2,10},{10... | collective-permute-start | bytes 491528 | tf_op jit(solution)/shard_map/ppermute | solution.py:651
  16.3 8.9 %collective-permute-start.7 = (f32[20,16,128]{2,1,0:T(8,128)S(1)}, f32[20,16,128]{2,1,0:T(8,128)S(1)}, u32[]{:S(2)}, u32[]{:S(2)}) collective-permute-start(f32[20,16,128]{2,1,0:T(8,128)S(1)} %get-tuple-element.71), channel_id=1, source_target_pairs={{0,24},{8,16},{16,8},{24,0},{1,25},{9,17},{17,9},{25,1},{2,26},{10... | collective-permute-start | bytes 491528 | tf_op jit(solution)/shard_map/ppermute | solution.py:650
  18.6 5.1 %collective-permute-start.8 = (f32[80,128]{1,0:T(8,128)S(1)}, f32[80,128]{1,0:T(8,128)S(1)}, u32[]{:S(2)}, u32[]{:S(2)}) collective-permute-start(f32[80,128]{1,0:T(8,128)S(1)} %get-tuple-element.72), channel_id=1, source_target_pairs={{0,1},{1,0},{2,3},{3,2},{4,5},{5,4},{6,7},{7,6},{8,9},{9,8},{10,11... | collective-permute-start | bytes 122888 | tf_op jit(solution)/shard_map/ppermute | solution.py:651
  20.8 3.9 %collective-permute-start.9 = (f32[80,128]{1,0:T(8,128)S(1)}, f32[80,128]{1,0:T(8,128)S(1)}, u32[]{:S(2)}, u32[]{:S(2)}) collective-permute-start(f32[80,128]{1,0:T(8,128)S(1)} %get-tuple-element.73), channel_id=1, source_target_pairs={{0,7},{1,2},{2,1},{3,4},{4,3},{5,6},{6,5},{7,0},{8,15},{9,10},{10,... | collective-permute-start | bytes 122888 | tf_op jit(solution)/shard_map/ppermute | solution.py:650
  26.3 19.0 %collective-permute-start.10 = (f32[20,16,128]{2,1,0:T(8,128)S(1)}, f32[20,16,128]{2,1,0:T(8,128)S(1)}, u32[]{:S(2)}, u32[]{:S(2)}) collective-permute-start(f32[20,16,128]{2,1,0:T(8,128)S(1)} %get-tuple-element.83), channel_id=1, source_target_pairs={{0,8},{8,0},{16,24},{24,16},{1,9},{9,1},{17,25},{25,17},{2,10},{10... | collective-permute-start | bytes 491528 | tf_op jit(solution)/shard_map/ppermute | solution.py:651
  26.3 19.0 %collective-permute-start.11 = (f32[20,16,128]{2,1,0:T(8,128)S(1)}, f32[20,16,128]{2,1,0:T(8,128)S(1)}, u32[]{:S(2)}, u32[]{:S(2)}) collective-permute-start(f32[20,16,128]{2,1,0:T(8,128)S(1)} %get-tuple-element.84), channel_id=1, source_target_pairs={{0,24},{8,16},{16,8},{24,0},{1,25},{9,17},{17,9},{25,1},{2,26},{10... | collective-permute-start | bytes 491528 | tf_op jit(solution)/shard_map/ppermute | solution.py:650
  27.8 6.1 %collective-permute-start.2 = (f32[9,16,128]{2,1,0:T(8,128)S(1)}, f32[9,16,128]{2,1,0:T(8,128)S(1)}, u32[]{:S(2)}, u32[]{:S(2)}) collective-permute-start(f32[9,16,128]{2,1,0:T(8,128)S(1)} %get-tuple-element.56), channel_id=1, source_target_pairs={{0,8},{8,0},{16,24},{24,16},{1,9},{9,1},{17,25},{25,17},{2,10},{10... | collective-permute-start | bytes 221192 | tf_op jit(solution)/shard_map/ppermute | solution.py:651
  28.4 12.3 %collective-permute-start.3 = (f32[9,16,128]{2,1,0:T(8,128)S(1)}, f32[9,16,128]{2,1,0:T(8,128)S(1)}, u32[]{:S(2)}, u32[]{:S(2)}) collective-permute-start(f32[9,16,128]{2,1,0:T(8,128)S(1)} %get-tuple-element.57), channel_id=1, source_target_pairs={{0,24},{8,16},{16,8},{24,0},{1,25},{9,17},{17,9},{25,1},{2,26},{10... | collective-permute-start | bytes 221192 | tf_op jit(solution)/shard_map/ppermute | solution.py:650
  30.2 15.0 %collective-permute-start.12 = (f32[80,128]{1,0:T(8,128)S(1)}, f32[80,128]{1,0:T(8,128)S(1)}, u32[]{:S(2)}, u32[]{:S(2)}) collective-permute-start(f32[80,128]{1,0:T(8,128)S(1)} %get-tuple-element.85), channel_id=1, source_target_pairs={{0,1},{1,0},{2,3},{3,2},{4,5},{5,4},{6,7},{7,6},{8,9},{9,8},{10,11... | collective-permute-start | bytes 122888 | tf_op jit(solution)/shard_map/ppermute | solution.py:651
  33.9 11.4 %collective-permute-start.13 = (f32[80,128]{1,0:T(8,128)S(1)}, f32[80,128]{1,0:T(8,128)S(1)}, u32[]{:S(2)}, u32[]{:S(2)}) collective-permute-start(f32[80,128]{1,0:T(8,128)S(1)} %get-tuple-element.86), channel_id=1, source_target_pairs={{0,7},{1,2},{2,1},{3,4},{4,3},{5,6},{6,5},{7,0},{8,15},{9,10},{10,... | collective-permute-start | bytes 122888 | tf_op jit(solution)/shard_map/ppermute | solution.py:650
